TPU v7x, 128 devices: a whole 4x4x4 slice. The times are simulated.
128 devices in a mesh: fsdp: 2 (over core), ctx: 64 (over z, x, y).
Axes of the slice: x: 4, y: 4, z: 4, core: 2. Of those that a mesh axis runs over, the one named last changes fastest.
Arguments:
- token_ids: int32 [2, 8192], P('fsdp', 'ctx'), may hold values from 0 to 511
- embedding: bfloat16 [512, 4096], P(None, 'fsdp'), may hold values from -5 to 5
- conv_taps: float32 [3, 3, 4096], replicated, may hold values from -2.5 to 2.5
- residues: float32 [4096, 16], replicated, may hold values from -1.2 to 1.2
- decays: float32 [4096, 16], replicated, may hold values from 2.4414062e-06 to 0.05
- filter_seed: int32 [4096, 16], replicated, may hold values from 0 to 4095
- skip_gain: float32 [4096], replicated, may hold values from 0.5 to 1.5
- cotangent: float32 [2, 4096, 8192], P('fsdp', None, 'ctx'), may hold values from -6 to 6
Outputs:
- mixer_out: float32 [2, 4096, 8192], P('fsdp', None, 'ctx')
- embed_grad: float32 [512, 4096], P(None, 'fsdp')
All inputs are finite; a program needn't handle non-finite values.
Results may differ from a plain program's by a relative error of at most 0.0006.
Values may be sent and summed in bfloat16 or wider, within the bound.
A program may use at most 320 MiB of HBM per device.

v0:
```python
import math

import jax
import jax.numpy as jnp
from jax import lax
from jax.sharding import PartitionSpec as P

PERIOD = 4096


HIGHEST = lax.Precision.HIGHEST
TWO_PI = 2.0 * math.pi


def from_behind(value, axis, steps):
    count = lax.axis_size(axis)
    leading, last = (max(0, -steps), min(count, count - steps))
    return lax.ppermute(value, axis, [(source, source + steps) for source in range(leading, last)])


def dft_tables(half_blocks, tok_block):
    full_blocks = 2 * half_blocks
    total_len = full_blocks * tok_block
    outer = (
        jnp.arange(half_blocks, dtype=jnp.int32)[:, None]
        * jnp.arange(full_blocks, dtype=jnp.int32)[None, :]
        % full_blocks
    )
    outer_angle = TWO_PI / full_blocks * outer.astype(jnp.float32)
    twist = (
        jnp.arange(full_blocks, dtype=jnp.int32)[:, None]
        * jnp.arange(tok_block, dtype=jnp.int32)[None, :]
        % total_len
    )
    twist_angle = TWO_PI / total_len * twist.astype(jnp.float32)
    inner = (
        jnp.arange(tok_block, dtype=jnp.int32)[:, None]
        * jnp.arange(tok_block, dtype=jnp.int32)[None, :]
        % tok_block
    )
    inner_angle = TWO_PI / tok_block * inner.astype(jnp.float32)
    return (
        jnp.cos(outer_angle),
        jnp.sin(outer_angle),
        jnp.cos(twist_angle),
        jnp.sin(twist_angle),
        jnp.cos(inner_angle),
        jnp.sin(inner_angle),
    )


def forward_dft(blocks, tables):
    outer_cos, outer_sin, twist_cos, twist_sin, inner_cos, inner_sin = tables
    part_real = jnp.einsum("bcst,sk->bckt", blocks, outer_cos, precision=HIGHEST)
    part_imag = -jnp.einsum("bcst,sk->bckt", blocks, outer_sin, precision=HIGHEST)
    turned_real = part_real * twist_cos + part_imag * twist_sin
    turned_imag = part_imag * twist_cos - part_real * twist_sin
    spec_real = jnp.einsum("bckt,tm->bckm", turned_real, inner_cos, precision=HIGHEST) + jnp.einsum(
        "bckt,tm->bckm", turned_imag, inner_sin, precision=HIGHEST
    )
    spec_imag = jnp.einsum("bckt,tm->bckm", turned_imag, inner_cos, precision=HIGHEST) - jnp.einsum(
        "bckt,tm->bckm", turned_real, inner_sin, precision=HIGHEST
    )
    return (spec_real, spec_imag)


def inverse_dft(prod_real, prod_imag, tables):
    outer_cos, outer_sin, twist_cos, twist_sin, inner_cos, inner_sin = tables
    total_len = outer_cos.shape[1] * inner_cos.shape[0]
    back_real = jnp.einsum("bckm,tm->bckt", prod_real, inner_cos, precision=HIGHEST) - jnp.einsum(
        "bckm,tm->bckt", prod_imag, inner_sin, precision=HIGHEST
    )
    back_imag = jnp.einsum("bckm,tm->bckt", prod_imag, inner_cos, precision=HIGHEST) + jnp.einsum(
        "bckm,tm->bckt", prod_real, inner_sin, precision=HIGHEST
    )
    turned_real = back_real * twist_cos - back_imag * twist_sin
    turned_imag = back_imag * twist_cos + back_real * twist_sin
    signal = jnp.einsum("bckt,sk->bcst", turned_real, outer_cos, precision=HIGHEST) - jnp.einsum(
        "bckt,sk->bcst", turned_imag, outer_sin, precision=HIGHEST
    )
    return signal / total_len


def apply_filter(spread, kernel_real, kernel_imag, tables, adjoint_sign):
    batch_rows = spread.shape[0]
    slab_size = spread.shape[1]
    half_blocks = tables[0].shape[0]
    tok_block = tables[4].shape[0]
    spec_real, spec_imag = forward_dft(
        spread.reshape(batch_rows, slab_size, half_blocks, tok_block), tables
    )
    prod_real = kernel_real * spec_real - adjoint_sign * kernel_imag * spec_imag
    prod_imag = kernel_real * spec_imag + adjoint_sign * kernel_imag * spec_real
    return inverse_dft(prod_real, prod_imag, tables).reshape(spread.shape)


def body(token_ids, embedding, conv_taps, residues, decays, filter_seed, skip_gain, cotangent):
    ctx_size = lax.axis_size("ctx")
    ctx_rank = lax.axis_index("ctx")
    model_width = conv_taps.shape[2]
    vocab_size = embedding.shape[0]
    tok_block = token_ids.shape[1]
    full_table = lax.all_gather(embedding, "fsdp", axis=1, tiled=True)
    gain_local = skip_gain[:, None]
    signal = jnp.swapaxes(jnp.take(full_table, token_ids, axis=0), 1, 2)
    before = from_behind(signal[:, :, tok_block - 2 :], "ctx", 1)
    extended = jnp.concatenate([before, signal], axis=2).astype(jnp.float32)

    def causal_mix(tap_set):
        return (
            tap_set[0][:, None] * extended[:, :, 2:]
            + tap_set[1][:, None] * extended[:, :, 1 : tok_block + 1]
            + tap_set[2][:, None] * extended[:, :, :tok_block]
        )

    query_stream = causal_mix(conv_taps[0])
    key_stream = causal_mix(conv_taps[1])
    value_stream = causal_mix(conv_taps[2])
    mixed_in = key_stream * value_stream
    grad_long = cotangent * query_stream
    seq_len = tok_block * ctx_size
    slab_size = model_width // ctx_size
    slab_start = ctx_rank * slab_size
    positions = jnp.arange(seq_len, dtype=jnp.int32)
    decay_rate = lax.dynamic_slice_in_dim(decays, slab_start, slab_size, 0)[:, :, None]
    seed_part = lax.dynamic_slice_in_dim(filter_seed, slab_start, slab_size, 0)[:, :, None]
    residue_part = lax.dynamic_slice_in_dim(residues, slab_start, slab_size, 0)[:, :, None]
    phase_int = seed_part * positions[None, None, :] % PERIOD
    weight = residue_part * jnp.sqrt(decay_rate + 1.0 / seq_len)
    kernel = jnp.sum(
        weight
        * jnp.exp(-decay_rate * positions.astype(jnp.float32)[None, None, :])
        * jnp.cos(TWO_PI / PERIOD * phase_int.astype(jnp.float32)),
        axis=1,
    )
    tables = dft_tables(ctx_size, tok_block)
    kernel_real, kernel_imag = forward_dft(
        kernel.reshape(1, slab_size, ctx_size, tok_block), tables
    )
    spread_mix, spread_grad = (
        lax.all_to_all(mixed_in, "ctx", split_axis=1, concat_axis=2, tiled=True),
        lax.all_to_all(grad_long, "ctx", split_axis=1, concat_axis=2, tiled=True),
    )
    conv_part = apply_filter(spread_mix, kernel_real, kernel_imag, tables, 1.0)
    corr_part = apply_filter(spread_grad, kernel_real, kernel_imag, tables, -1.0)
    conv_out, correlated = (
        lax.all_to_all(conv_part, "ctx", split_axis=2, concat_axis=1, tiled=True),
        lax.all_to_all(corr_part, "ctx", split_axis=2, concat_axis=1, tiled=True),
    )
    long_out = conv_out + gain_local * mixed_in
    mixer_local = query_stream * long_out
    grad_query = cotangent * long_out
    grad_mixed = correlated + gain_local * grad_long
    grad_key = grad_mixed * value_stream
    grad_value = grad_mixed * key_stream

    def tap_term(tap_index):
        return (
            conv_taps[0][tap_index][:, None] * grad_query
            + conv_taps[1][tap_index][:, None] * grad_key
            + conv_taps[2][tap_index][:, None] * grad_value
        )

    first_term = tap_term(0)
    second_term = tap_term(1)
    third_term = tap_term(2)
    next_rows = from_behind(jnp.stack([second_term[:, :, :2], third_term[:, :, :2]]), "ctx", -1)
    grad_signal = (
        first_term
        + jnp.concatenate([second_term, next_rows[0]], axis=2)[:, :, 1 : tok_block + 1]
        + jnp.concatenate([third_term, next_rows[1]], axis=2)[:, :, 2 : tok_block + 2]
    )
    one_hot = (
        token_ids[:, :, None] == jnp.arange(vocab_size, dtype=jnp.int32)[None, None, :]
    ).astype(jnp.float32)
    partial_grad = jnp.einsum("btv,bct->vc", one_hot, grad_signal, precision=HIGHEST)
    half_grad = lax.psum_scatter(partial_grad, "fsdp", scatter_dimension=1, tiled=True)
    embed_grad = lax.psum(half_grad, "ctx")
    return (mixer_local, embed_grad)


def solution(mesh):
    placed = (P("fsdp", "ctx"), P(None, "fsdp"), P(), P(), P(), P(), P(), P("fsdp", None, "ctx"))
    return jax.shard_map(
        body,
        mesh=mesh,
        in_specs=placed,
        out_specs=(P("fsdp", None, "ctx"), P(None, "fsdp")),
        check_vma=False,
    )
```

profile of v0, /device:TPU:0, one launch (start us, length us, event | category | flops | bytes accessed | tf_op | source)
XLA Modules:
  0.0 764.9 jit_solution(1966881312093857230)
XLA Ops:
  12.0 16.5 %all-gather.2.cloned.1.call-done = bf16[512,4096]{1,0:T(8,128)(2,1)} async-done(((bf16[512,2048]{1,0:T(8,128)(2,1)}), bf16[512,4096]{1,0:T(8,128)(2,1)}) %all-gather.2.cloned.1.call-update) | async-done | bytes 4194320 | tf_op jit(solution)/shard_map/all_gather | solution.py:103
  28.5 4.9 gather_fusion
  34.2 4.1 collective-permute-start
  41.7 4.8 fusion.348
  46.5 5.6 copy.93
  52.2 10.4 %all-to-all-start.2 = ((f32[1,4096,128]{2,0,1:T(1,128)}), f32[1,4096,128]{2,0,1:T(1,128)S(1)}, u32[]{:S(2)}, u32[]{:S(2)}) async-start(f32[1,4096,128]{2,0,1:T(1,128)} %copy.93), calls=%async_computation.2 | async-start | bytes 4194304 | tf_op jit(solution)/shard_map/all_to_all | solution.py:142
  62.6 133.4 %fusion.5 = f32[64,8192]{1,0:T(8,128)S(1)} fusion(s32[64,16]{1,0:T(8,128)S(1)} %copy.84, f32[8192]{0:T(1024)S(1)} %copy-done.32, f32[64,16]{1,0:T(8,128)S(1)} %copy.83, f32[64,16]{1,0:T(8,128)S(1)} %copy.82), kind=kLoop, calls=%fused_computation.9 | loop fusion | flops 150470656 | bytes 2142208 | tf_op jit(solution)/shard_map/reduce_sum | solution.py:130
  196.8 3.7 fusion.175
  200.5 3.7 fusion.181
  204.2 5.8 fusion.27
  210.0 5.6 fusion.29
  215.6 5.7 copy.85
  221.2 10.9 %all-to-all-start = ((f32[1,4096,128]{2,0,1:T(1,128)}), f32[1,4096,128]{2,0,1:T(1,128)}, u32[]{:S(2)}, u32[]{:S(2)}) async-start(f32[1,4096,128]{2,0,1:T(1,128)} %copy.85), calls=%async_computation | async-start | bytes 4194304 | tf_op jit(solution)/shard_map/all_to_all | solution.py:141
  232.2 8.8 %fusion.58 = f32[64,128,128]{2,1,0:T(8,128)} fusion(f32[64,128,128]{2,1,0:T(8,128)} %fusion.27, f32[128,64,128]{2,0,1:T(8,128)} %copy-done.6, f32[128,64,128]{2,0,1:T(8,128)} %copy-done.4, f32[128,128]{1,0:T(8,128)S(1)} %get-tuple-element.45, f32[128,128]{1,0:T(8,128)S(1)} %get-tuple-element.46), kind=kOutput, calls=%fused_computation.76 | convolution fusion | flops 1616084992 | bytes 16908288 | tf_op jit(solution)/shard_map/bckt,tm->bckm/dot_general | solution.py:61
  242.0 5.7 fusion.55
  247.7 7.0 fusion.81
  254.7 7.3 fusion.83
  262.1 6.3 fusion.85
  268.4 6.3 fusion.87
  274.7 4.3 fusion.19
  279.1 4.1 fusion.21
  283.2 4.2 fusion.9
  287.4 5.7 fusion.11
  293.1 6.0 fusion.64
  299.1 5.8 fusion.61
  304.9 5.8 fusion.70
  310.8 19.4 %multiply_add_fusion = (f32[64,128,128]{2,1,0:T(8,128)}, f32[64,128,128]{2,1,0:T(8,128)}, f32[64,128,128]{2,1,0:T(8,128)}, f32[64,128,128]{2,1,0:T(8,128)}) fusion(f32[64,128,128]{2,1,0:T(8,128)} %fusion.55, f32[64,128,128]{2,1,0:T(8,128)} %fusion.70, f32[64,128,128]{2,1,0:T(8,128)} %fusion.58, f32[64,128,128]{2,1,0:T(8,128)} %fusion.64, ...), kind=kOutput, calls=%fused_computation.63 | convolution fusion | flops 1629716480 | bytes 50462720 | tf_op jit(solution)/shard_map/bckt,tm->bckm/dot_general | solution.py:58
  330.1 6.5 fusion.147
  336.6 3.8 fusion.149
  340.5 3.8 convolution_add_fusion
  344.3 3.8 convolution_subtract_fusion
  348.0 3.2 fusion.39
  351.2 3.1 multiply_bitcast_fusion
  354.3 2.8 copy.101
  357.7 38.4 %reduce.2 = f32[8192,64]{1,0:T(8,128)} reduce(f32[8192,1,64]{2,1,0:T(1,128)} %bitcast.330, f32[]{:T(128)} %broadcast.309), dimensions={1}, to_apply=%bitcast.304.reduce_sub_computation | reduce | bytes 4194308
  396.1 5.5 reshape.405
  401.6 10.7 %all-to-all-start.3 = ((f32[64,1,8192]{2,1,0:T(1,128)}), f32[64,1,8192]{2,1,0:T(1,128)}, u32[]{:S(2)}, u32[]{:S(2)}) async-start(f32[64,1,8192]{2,1,0:T(1,128)} %reshape.405), calls=%async_computation.3 | async-start | bytes 4194304 | tf_op jit(solution)/shard_map/all_to_all | solution.py:148
  412.3 6.4 fusion.155
  418.7 3.8 fusion.153
  422.5 3.8 convolution_subtract_fusion.1
  426.3 3.8 convolution_add_fusion.1
  430.1 3.2 fusion.47
  433.3 3.1 multiply_bitcast_fusion.1
  436.4 2.8 copy.100
  439.2 38.4 %reduce = f32[8192,64]{1,0:T(8,128)} reduce(f32[8192,1,64]{2,1,0:T(1,128)} %bitcast.331, f32[]{:T(128)} %broadcast.309), dimensions={1}, to_apply=%bitcast.302.reduce_sub_computation | reduce | bytes 4194308
  477.6 5.5 reshape.403
  483.1 10.5 %all-to-all-start.1 = ((f32[64,1,8192]{2,1,0:T(1,128)}), f32[64,1,8192]{2,1,0:T(1,128)}, u32[]{:S(2)}, u32[]{:S(2)}) async-start(f32[64,1,8192]{2,1,0:T(1,128)} %reshape.403), calls=%async_computation.1 | async-start | bytes 4194304 | tf_op jit(solution)/shard_map/all_to_all | solution.py:147
  494.0 7.5 reduce.3
  501.6 6.6 reshape.406
  508.1 9.1 %copy.96 = f32[1,64,8192]{2,0,1:T(1,128)S(1)} copy(f32[1,64,8192]{1,0,2:T(1,128)} %bitcast.328) | data formatting | bytes 4194304 | tf_op jit(solution)/shard_map/all_to_all | solution.py:148
  517.2 2.5 copy.97
  519.8 2.9 copy.98
  522.7 7.5 reduce.1
  530.2 6.8 reshape.404
  536.9 10.5 %copy.88 = f32[1,64,8192]{2,0,1:T(1,128)} copy(f32[1,64,8192]{1,0,2:T(1,128)} %bitcast.329) | data formatting | bytes 4194304 | tf_op jit(solution)/shard_map/all_to_all | solution.py:147
  547.4 4.3 copy.89
  551.7 2.9 copy.90
  554.7 10.9 %multiply_add_fusion.3 = (f32[1,4096,128]{1,2,0:T(8,128)}, f32[1,4096,128]{1,2,0:T(8,128)}, f32[1,4096,128]{1,2,0:T(8,128)}, f32[1,4096,128]{1,2,0:T(8,128)}, f32[1,4096,128]{1,2,0:T(8,128)}) fusion(f32[4096]{0:T(1024)S(1)} %bitcast.354, f32[4096]{0:T(1024)S(1)} %bitcast.350, f32[4096]{0:T(1024)S(1)} %bitcast.352, f32[1,4096,128]{1,2,0:T(8,128)S(1)} %copy-done.13, ...), kind=kLoop, calls=%fused_computation.102 | loop fusion | flops 6815744 | bytes 27328512 | tf_op jit(solution)/shard_map/add | solution.py:159
  566.6 3.5 multiply_add_fusion.2
  571.6 4.9 collective-permute-done.1
  576.5 6.5 fusion.75
  583.0 24.6 %reduce-scatter.2.cloned.1.call-done = f32[512,2048]{1,0:T(8,128)} async-done(((f32[512,4096]{1,0:T(8,128)}), f32[512,2048]{1,0:T(8,128)}) %reduce-scatter.2.cloned.1.call-update) | async-done | bytes 4194320 | tf_op jit(solution)/shard_map/reduce_scatter | solution.py:177
  609.5 144.1 %all-reduce.2.cloned.1.call-done = f32[512,2048]{1,0:T(8,128)} async-done(((f32[512,2048]{1,0:T(8,128)}), f32[512,2048]{1,0:T(8,128)}) %all-reduce.2.cloned.1.call-update) | async-done | bytes 4194320 | tf_op jit(solution)/shard_map/psum | solution.py:178
  753.5 4.7 copy.120
  (104 shorter events, 15.9 us)
Async XLA Ops:
  7.2 31.2 %copy-start = (s32[4096,16]{0,1:T(8,128)S(1)}, s32[4096,16]{0,1:T(8,128)}, u32[]{:S(2)}) copy-start(s32[4096,16]{0,1:T(8,128)} %param.13) | copy-start | bytes 786436
  7.2 21.3 %all-gather.2.cloned.1.call-start = ((), (), s32[]{:S(2)}) async-start(), calls=%async_computation.5 | async-start | bytes 6291456 | tf_op jit(solution)/shard_map/all_gather | solution.py:103
  11.9 29.8 %copy-start.20 = (f32[1,1,4096]{2,1,0:T(1,128)}, f32[1,1,4096]{2,1,0:T(1,128)S(1)}, u32[]{:S(2)}) copy-start(f32[1,1,4096]{2,1,0:T(1,128)S(1)} %get-tuple-element.36) | copy-start | bytes 49156
  11.9 29.8 %copy-start.22 = (f32[1,1,4096]{2,1,0:T(1,128)}, f32[1,1,4096]{2,1,0:T(1,128)S(1)}, u32[]{:S(2)}) copy-start(f32[1,1,4096]{2,1,0:T(1,128)S(1)} %get-tuple-element.38) | copy-start | bytes 49156
  11.9 29.8 %copy-start.24 = (f32[1,1,4096]{2,1,0:T(1,128)}, f32[1,1,4096]{2,1,0:T(1,128)S(1)}, u32[]{:S(2)}) copy-start(f32[1,1,4096]{2,1,0:T(1,128)S(1)} %get-tuple-element.41) | copy-start | bytes 49156
  11.9 29.8 %copy-start.26 = (f32[1,1,4096]{2,1,0:T(1,128)}, f32[1,1,4096]{2,1,0:T(1,128)S(1)}, u32[]{:S(2)}) copy-start(f32[1,1,4096]{2,1,0:T(1,128)S(1)} %get-tuple-element.34) | copy-start | bytes 49156
  11.9 29.8 %copy-start.28 = (f32[1,1,4096]{2,1,0:T(1,128)}, f32[1,1,4096]{2,1,0:T(1,128)S(1)}, u32[]{:S(2)}) copy-start(f32[1,1,4096]{2,1,0:T(1,128)S(1)} %get-tuple-element.35) | copy-start | bytes 49156
  12.0 29.8 %copy-start.30 = (f32[1,1,4096]{2,1,0:T(1,128)}, f32[1,1,4096]{2,1,0:T(1,128)S(1)}, u32[]{:S(2)}) copy-start(f32[1,1,4096]{2,1,0:T(1,128)S(1)} %get-tuple-element.40) | copy-start | bytes 49156
  34.2 6.3 collective-permute-start
  40.6 6.0 copy-start.12
  46.5 16.1 %copy-start.32 = (f32[8192]{0:T(1024)S(1)}, f32[8192]{0:T(1024)}, u32[]{:S(2)}) copy-start(f32[8192]{0:T(1024)} %iota_convert_fusion) | copy-start | bytes 98308
  52.2 169.0 %all-to-all-start.2 = ((f32[1,4096,128]{2,0,1:T(1,128)}), f32[1,4096,128]{2,0,1:T(1,128)S(1)}, u32[]{:S(2)}, u32[]{:S(2)}) async-start(f32[1,4096,128]{2,0,1:T(1,128)} %copy.93), calls=%async_computation.2 | async-start | bytes 4194304 | tf_op jit(solution)/shard_map/all_to_all | solution.py:142
  200.5 9.5 %copy-start.4 = (f32[128,64,128]{2,0,1:T(8,128)}, f32[128,64,128]{2,0,1:T(8,128)S(1)}, u32[]{:S(2)}) copy-start(f32[128,64,128]{2,0,1:T(8,128)S(1)} %fusion.175) | copy-start | bytes 12582916
  204.2 5.8 copy-start.6
  221.2 40.8 %all-to-all-start = ((f32[1,4096,128]{2,0,1:T(1,128)}), f32[1,4096,128]{2,0,1:T(1,128)}, u32[]{:S(2)}, u32[]{:S(2)}) async-start(f32[1,4096,128]{2,0,1:T(1,128)} %copy.85), calls=%async_computation | async-start | bytes 4194304 | tf_op jit(solution)/shard_map/all_to_all | solution.py:141
  232.2 8.8 %copy-start.5 = (f32[128,64,128]{2,0,1:T(8,128)S(1)}, f32[128,64,128]{2,0,1:T(8,128)}, u32[]{:S(2)}) copy-start(f32[128,64,128]{2,0,1:T(8,128)} %copy-done.4) | copy-start | bytes 12582916
  232.2 8.8 %copy-start.7 = (f32[128,64,128]{2,0,1:T(8,128)S(1)}, f32[128,64,128]{2,0,1:T(8,128)}, u32[]{:S(2)}) copy-start(f32[128,64,128]{2,0,1:T(8,128)} %copy-done.6) | copy-start | bytes 12582916
  232.2 9.8 %copy-start.17 = (f32[64,128,128]{2,1,0:T(8,128)S(1)}, f32[64,128,128]{2,1,0:T(8,128)}, u32[]{:S(2)}) copy-start(f32[64,128,128]{2,1,0:T(8,128)} %fusion.29) | copy-start | bytes 12582916
  279.1 4.2 copy-start.2
  279.1 4.2 copy-start.3
  330.1 6.5 copy-start.11
  340.5 3.8 copy-start.10
  401.6 81.5 %all-to-all-start.3 = ((f32[64,1,8192]{2,1,0:T(1,128)}), f32[64,1,8192]{2,1,0:T(1,128)}, u32[]{:S(2)}, u32[]{:S(2)}) async-start(f32[64,1,8192]{2,1,0:T(1,128)} %reshape.405), calls=%async_computation.3 | async-start | bytes 4194304 | tf_op jit(solution)/shard_map/all_to_all | solution.py:148
  412.3 6.5 copy-start.9
  422.5 3.8 copy-start.8
  483.1 39.6 %all-to-all-start.1 = ((f32[64,1,8192]{2,1,0:T(1,128)}), f32[64,1,8192]{2,1,0:T(1,128)}, u32[]{:S(2)}, u32[]{:S(2)}) async-start(f32[64,1,8192]{2,1,0:T(1,128)} %reshape.403), calls=%async_computation.1 | async-start | bytes 4194304 | tf_op jit(solution)/shard_map/all_to_all | solution.py:147
  493.6 114.0 %reduce-scatter.2.cloned.1.call-start = ((), (), s32[]{:S(2)}) async-start(), calls=%async_computation.6 | async-start | bytes 12582912 | tf_op jit(solution)/shard_map/reduce_scatter | solution.py:177
  547.4 7.2 copy-start.13
  547.4 7.2 copy-start.33
  554.6 11.8 %copy-start.21 = (f32[1,1,4096]{2,1,0:T(1,128)S(1)}, f32[1,1,4096]{2,1,0:T(1,128)}, u32[]{:S(2)}) copy-start(f32[1,1,4096]{2,1,0:T(1,128)} %copy-done.20) | copy-start | bytes 49156
  554.6 11.8 %copy-start.23 = (f32[1,1,4096]{2,1,0:T(1,128)S(1)}, f32[1,1,4096]{2,1,0:T(1,128)}, u32[]{:S(2)}) copy-start(f32[1,1,4096]{2,1,0:T(1,128)} %copy-done.22) | copy-start | bytes 49156
  554.7 11.8 %copy-start.25 = (f32[1,1,4096]{2,1,0:T(1,128)S(1)}, f32[1,1,4096]{2,1,0:T(1,128)}, u32[]{:S(2)}) copy-start(f32[1,1,4096]{2,1,0:T(1,128)} %copy-done.24) | copy-start | bytes 49156
  566.5 9.9 %copy-start.14 = (f32[1,4096,128]{1,2,0:T(8,128)S(1)}, f32[1,4096,128]{1,2,0:T(8,128)}, u32[]{:S(2)}) copy-start(f32[1,4096,128]{1,2,0:T(8,128)} %get-tuple-element.15) | copy-start | bytes 6291460
  566.5 9.9 %copy-start.15 = (f32[1,4096,128]{1,2,0:T(8,128)S(1)}, f32[1,4096,128]{1,2,0:T(8,128)}, u32[]{:S(2)}) copy-start(f32[1,4096,128]{1,2,0:T(8,128)} %get-tuple-element.16) | copy-start | bytes 6291460
  566.5 9.9 %copy-start.16 = (f32[1,4096,128]{1,2,0:T(8,128)S(1)}, f32[1,4096,128]{1,2,0:T(8,128)}, u32[]{:S(2)}) copy-start(f32[1,4096,128]{1,2,0:T(8,128)} %get-tuple-element.17) | copy-start | bytes 6291460
  566.5 9.9 %copy-start.18 = (f32[1,4096,128]{1,2,0:T(8,128)S(1)}, f32[1,4096,128]{1,2,0:T(8,128)}, u32[]{:S(2)}) copy-start(f32[1,4096,128]{1,2,0:T(8,128)} %get-tuple-element.14) | copy-start | bytes 6291460
  566.5 9.9 %copy-start.27 = (f32[1,1,4096]{2,1,0:T(1,128)S(1)}, f32[1,1,4096]{2,1,0:T(1,128)}, u32[]{:S(2)}) copy-start(f32[1,1,4096]{2,1,0:T(1,128)} %copy-done.26) | copy-start | bytes 49156
  566.5 9.9 %copy-start.29 = (f32[1,1,4096]{2,1,0:T(1,128)S(1)}, f32[1,1,4096]{2,1,0:T(1,128)}, u32[]{:S(2)}) copy-start(f32[1,1,4096]{2,1,0:T(1,128)} %copy-done.28) | copy-start | bytes 49156
  566.6 9.9 %copy-start.31 = (f32[1,1,4096]{2,1,0:T(1,128)S(1)}, f32[1,1,4096]{2,1,0:T(1,128)}, u32[]{:S(2)}) copy-start(f32[1,1,4096]{2,1,0:T(1,128)} %copy-done.30) | copy-start | bytes 49156
  566.6 9.9 %copy-start.34 = (s32[1,128]{1,0:T(1,128)S(1)}, s32[1,128]{1,0:T(1,128)}, u32[]{:S(2)}) copy-start(s32[1,128]{1,0:T(1,128)} %param.8) | copy-start | bytes 1540
  570.1 6.3 collective-permute-start.1
  583.0 24.6 %copy-start.19 = (f32[1,4096,128]{1,2,0:T(8,128)S(1)}, f32[1,4096,128]{1,2,0:T(8,128)}, u32[]{:S(2)}) copy-start(f32[1,4096,128]{1,2,0:T(8,128)} %get-tuple-element.29) | copy-start | bytes 6291460
  583.0 170.5 %all-reduce.2.cloned.1.call-start = ((), (), s32[]{:S(2)}) async-start(), calls=%async_computation.7 | async-start | bytes 8388608 | tf_op jit(solution)/shard_map/psum | solution.py:178
  607.6 150.6 %copy-start.1 = (s32[4096,16]{0,1:T(8,128)S(1)}, s32[4096,16]{0,1:T(8,128)}, u32[]{:S(2)}) copy-start(s32[4096,16]{0,1:T(8,128)} %param.13) | copy-start | bytes 786436
Sparse Core Ops, SparseCore 0:
  9.7 18.7 all-gather.1
  583.1 24.4 reduce-scatter.1
  613.4 140.0 all-reduce.1
where the time goes:
time: 772 us; the launch traced here: 765 us
  other arithmetic  249 us (32%)
  waiting for transfers between devices  191 us (25%)
  matrix products  170 us (22%)
  local copies, waits for them, and re-layouts  92 us (12%)
  starting transfers between devices  48.6 us (6%)
  between operations  14.7 us (2%)
    psum x1, waiting for transfers between devices, body(): embed_grad = lax.psum(half_grad, 'ctx')  144 us
    reduce_sum x1, other arithmetic, body(): jnp.sum(weight * jnp.exp(-decay_rate * positions.astype(jnp.float32)[None...  133 us
    unnamed x2, other arithmetic  76.8 us
    unnamed x79, local copies, waits for them, and re-layouts  34.9 us
    dot_general x3, matrix products, forward_dft(): jnp.einsum('bckt,tm->bckm', turned_imag, inner_sin, precision=HIGHEST)  30.9 us
    reduce_scatter x1, waiting for transfers between devices, body(): lax.psum_scatter(partial_grad, 'fsdp', scatter_dimension=1, tiled=True)  24.6 us
    dot_general x3, matrix products, forward_dft(): jnp.einsum('bckt,tm->bckm', turned_imag, inner_cos, precision=HIGHEST)  20.6 us
    all_to_all x3, local copies, waits for them, and re-layouts, body(): lax.all_to_all(conv_part, 'ctx', split_axis=2, concat_axis=1, tiled=True)  17.7 us
  transfers between devices with their start and end apart: 9, of which 4 were waited for; matrix products, arithmetic and copies ran while one was open for 39% of the time, Pallas kernels for 0%

commit v1 on v0

v1 whole, which is shorter than its diff:
```python
import functools
import math

import jax
import jax.numpy as jnp
from jax import lax
from jax.experimental import pallas as pl
from jax.experimental.pallas import tpu as pltpu
from jax.sharding import PartitionSpec as P

PERIOD = 4096
F32 = jnp.float32
BF16 = jnp.bfloat16
LANES = 128
GROUP = 8


def iota(shape, dim):
    return lax.broadcasted_iota(jnp.int32, shape, dim)


def split(value):
    high = value.astype(BF16)
    return high, (value - high.astype(F32)).astype(BF16)


def cis(phase):
    quarter = PERIOD // 4
    turn = (phase + quarter // 2) // quarter
    a = (phase - turn * quarter).astype(F32) * (2.0 * math.pi / PERIOD)
    b = a * a
    s = a * (1.0 + b * (-1 / 6 + b * (1 / 120 + b * (-1 / 5040 + b * (1 / 362880)))))
    c = 1.0 + b * (-0.5 + b * (1 / 24 + b * (-1 / 720 + b * (1 / 40320))))
    odd = turn % 2 == 1
    re = jnp.where(odd, s, c)
    im = jnp.where(odd, c, s)
    re = jnp.where((turn == 1) | (turn == 2), -re, re)
    im = jnp.where((turn == 2) | (turn == 3), -im, im)
    return re, im


def power(rate, seed, steps):
    mag = jnp.exp(-rate * steps.astype(F32))
    re, im = cis((seed * steps) % PERIOD)
    return mag * re, mag * im


def nn(a, b):
    return jnp.dot(a, b, preferred_element_type=F32)


def nt(a, b):
    return lax.dot_general(a, b, (((1,), (1,)), ((), ())), preferred_element_type=F32)


def three(dot, left, right):
    left_high, left_low = left
    right_high, right_low = right
    rows = left_high.shape[0]
    both = dot(jnp.concatenate([left_high, left_low], axis=0), right_high)
    return both[:rows] + both[rows:] + dot(left_high, right_low)


def block_kernel(
    chunks, modes, seq_len,
    tok, table, taps, residues, decays, seeds, cot,
    mixed_out, table_grad,
    query, key, value, mix, long_out,
    bank, toeplitz, diag, state_rows,
):
    rows = tok.shape[0]
    slab = table.shape[0]
    vocab = table.shape[1]
    groups = slab // GROUP
    wide = GROUP * modes

    spread = (iota((slab * modes, slab), 0) // modes == iota((slab * modes, slab), 1)).astype(F32)
    pick = iota((slab * modes, modes), 0) % modes == iota((slab * modes, modes), 1)

    def column(part):
        wide_part = jnp.dot(spread, part, precision=lax.Precision.HIGHEST, preferred_element_type=F32)
        return jnp.sum(jnp.where(pick, wide_part, 0.0), axis=1, keepdims=True)

    rate = column(decays[...])
    seed = column(seeds[...].astype(F32))
    res = column(residues[...])
    weight = res * jnp.sqrt(rate + 1.0 / seq_len)
    seed_int = (seed + 0.5).astype(jnp.int32)
    rate_b = jnp.broadcast_to(rate, (slab * modes, LANES))
    seed_b = jnp.broadcast_to(seed_int, (slab * modes, LANES))
    lane = iota((slab * modes, LANES), 1)
    up = power(rate_b, seed_b, lane)
    down = power(rate_b, seed_b, LANES - 1 - lane)
    for place, part in enumerate((*up, *down)):
        high, low = split(part)
        bank[2 * place] = high
        bank[2 * place + 1] = low
    kernel_head = jnp.sum((up[0] * weight).reshape(slab, modes, LANES), axis=1)
    kernel_head = kernel_head + jnp.where(iota((slab, LANES), 1) == 0, taps[9], 0.0)

    upper = iota((LANES, LANES), 1) >= iota((LANES, LANES), 0)
    for c in range(slab):
        line = jnp.broadcast_to(kernel_head[c : c + 1], (LANES, LANES))
        rolled = pltpu.roll(line, 0, 1, stride=1, stride_axis=0)
        high, low = split(jnp.where(upper, rolled, 0.0))
        toeplitz[0, c] = high
        toeplitz[1, c] = low

    eye = iota((wide, LANES), 0) == iota((wide, LANES), 1)
    step_row = iota((8, LANES), 0)
    steps = jnp.where(step_row == 6, 1, LANES * (1 << jnp.minimum(step_row, 5)))
    for g in range(groups):
        def row(part):
            piece = jnp.broadcast_to(part[g * wide : (g + 1) * wide], (wide, LANES))
            return jnp.sum(jnp.where(eye, piece, 0.0), axis=0, keepdims=True)

        rate_row = jnp.broadcast_to(row(rate), (8, LANES))
        seed_row = jnp.broadcast_to((row(seed) + 0.5).astype(jnp.int32), (8, LANES))
        weight_row = row(weight)
        re, im = power(rate_row, seed_row, steps)
        scale = jnp.where(step_row == 6, jnp.broadcast_to(weight_row, (8, LANES)), 1.0)
        state_rows[g, 0] = re * scale
        state_rows[g, 1] = im * scale

    diag[...] = jnp.zeros_like(diag)

    lane_c = iota((slab, LANES), 1)
    vocab_row = iota((vocab, LANES), 0)

    def one_hot(r):
        return jnp.where(vocab_row == tok[pl.ds(r, 1), :], 1.0, 0.0).astype(BF16)

    UNROLL = 4

    def gather(step, carry):
        last_one, last_two = carry
        r0 = step * UNROLL
        hot = jnp.concatenate([one_hot(r0 + i) for i in range(UNROLL)], axis=1)
        found = nn(table[...], hot)
        fresh = (r0 % chunks) == 0
        last_one = jnp.where(fresh, 0.0, last_one)
        last_two = jnp.where(fresh, 0.0, last_two)
        for i in range(UNROLL):
            x = found[:, i * LANES : (i + 1) * LANES]
            one = pltpu.roll(x, 1, 1)
            two = pltpu.roll(x, 2, 1)
            x1 = jnp.where(lane_c < 1, last_one, one)
            x2 = jnp.where(lane_c < 2, last_two, two)
            last_one, last_two = one, two
            q, k, v = (taps[3 * s] * x + taps[3 * s + 1] * x1 + taps[3 * s + 2] * x2 for s in range(3))
            at = pl.ds(pl.multiple_of((r0 + i) * slab, slab), slab)
            query[at, :] = q
            key[at, :] = k
            value[at, :] = v
            mix[at, :] = k * v
        return last_one, last_two

    zero = jnp.zeros((slab, LANES), F32)
    lax.fori_loop(0, rows // UNROLL, gather, (zero, zero))

    row_in_seq = iota((rows, LANES), 0) % chunks

    def scan(re, im, g, backward):
        for j in range(max(1, (chunks - 1).bit_length())):
            shift = 1 << j
            amount = rows - shift if backward else shift
            keep = row_in_seq < chunks - shift if backward else row_in_seq >= shift
            old_re = jnp.where(keep, pltpu.roll(re, amount, 0), 0.0)
            old_im = jnp.where(keep, pltpu.roll(im, amount, 0), 0.0)
            a, b = state_rows[g, 0, j : j + 1, :], state_rows[g, 1, j : j + 1, :]
            re, im = re + a * old_re - b * old_im, im + a * old_im + b * old_re
        amount = rows - 1 if backward else 1
        keep = row_in_seq < chunks - 1 if backward else row_in_seq >= 1
        re = jnp.where(keep, pltpu.roll(re, amount, 0), 0.0)
        im = jnp.where(keep, pltpu.roll(im, amount, 0), 0.0)
        a, b = state_rows[g, 0, 6:7, :], state_rows[g, 1, 6:7, :]
        return a * re - b * im, -(a * im + b * re)

    def long_conv(source, target, backward):
        enter, leave = (0, 2) if backward else (2, 0)

        def per_group(g, _):
            base = g * GROUP
            for side, first in enumerate((enter, leave)):
                for c in range(GROUP):
                    at = pl.ds(pl.multiple_of(g * wide + c * modes, modes), modes)
                    for half in range(2):
                        spot = slice(half * wide + c * modes, half * wide + (c + 1) * modes)
                        for part in range(2):
                            diag[side, part, spot, c * LANES : (c + 1) * LANES] = bank[
                                2 * (first + half) + part, at, :
                            ]
            local = jnp.zeros((rows, 2 * wide), F32)
            for c in range(GROUP):
                u = split(source[pl.ds(base + c, rows, stride=slab), :])
                at = slice(c * LANES, (c + 1) * LANES)
                local = local + three(nt, u, (diag[0, 0, :, at], diag[0, 1, :, at]))
            re, im = scan(local[:, :wide], local[:, wide:], g, backward)
            state = split(jnp.concatenate([re, im], axis=1))
            for c in range(GROUP):
                u = split(source[pl.ds(base + c, rows, stride=slab), :])
                at = slice(c * LANES, (c + 1) * LANES)
                band = (toeplitz[0, base + c], toeplitz[1, base + c])
                out = three(nt if backward else nn, u, band)
                out = out + three(nn, state, (diag[1, 0, :, at], diag[1, 1, :, at]))
                target[pl.ds(base + c, rows, stride=slab), :] = out
            return 0

        lax.fori_loop(0, groups, per_group, 0)

    long_conv(mix, long_out, False)

    def emit(r, _):
        at = pl.ds(pl.multiple_of(r * slab, slab), slab)
        q = query[at, :]
        mixed_out[at, :] = q * long_out[at, :]
        mix[at, :] = cot[at, :] * q
        return 0

    lax.fori_loop(0, rows, emit, 0, unroll=4)

    grad_mixed = query
    long_conv(mix, grad_mixed, True)

    def scatter(step, carry):
        next_one, next_two, total = carry
        r0 = rows - UNROLL - step * UNROLL
        fresh = (r0 % chunks) == chunks - UNROLL
        next_one = jnp.where(fresh, 0.0, next_one)
        next_two = jnp.where(fresh, 0.0, next_two)
        pieces = [None] * UNROLL
        for i in reversed(range(UNROLL)):
            at = pl.ds(pl.multiple_of((r0 + i) * slab, slab), slab)
            gm = grad_mixed[at, :]
            gq = cot[at, :] * long_out[at, :]
            gk = gm * value[at, :]
            gv = gm * key[at, :]
            zeroth, first, second = (taps[j] * gq + taps[3 + j] * gk + taps[6 + j] * gv for j in range(3))
            one = pltpu.roll(first, LANES - 1, 1)
            two = pltpu.roll(second, LANES - 2, 1)
            gx = (
                zeroth
                + jnp.where(lane_c >= LANES - 1, next_one, one)
                + jnp.where(lane_c >= LANES - 2, next_two, two)
            )
            next_one, next_two = one, two
            pieces[i] = jnp.concatenate(split(gx), axis=0)
        hot = jnp.concatenate([one_hot(r0 + i) for i in range(UNROLL)], axis=1)
        return next_one, next_two, total + nt(jnp.concatenate(pieces, axis=1), hot)

    _, _, total = lax.fori_loop(
        0, rows // UNROLL, scatter, (zero, zero, jnp.zeros((2 * slab, vocab), F32))
    )
    table_grad[...] = total[:slab] + total[slab:]


def run_block(tok, table, taps, residues, decays, seeds, cot, chunks, seq_len):
    rows = tok.shape[0]
    slab, vocab = table.shape
    modes = residues.shape[1]
    tall = rows * slab
    vmem = pl.BlockSpec(memory_space=pltpu.VMEM)
    return pl.pallas_call(
        functools.partial(block_kernel, chunks, modes, seq_len),
        out_shape=(
            jax.ShapeDtypeStruct((tall, LANES), F32),
            jax.ShapeDtypeStruct((slab, vocab), F32),
        ),
        in_specs=[vmem] * 7,
        out_specs=(vmem, vmem),
        scratch_shapes=[pltpu.VMEM((tall, LANES), F32)] * 5
        + [
            pltpu.VMEM((8, slab * modes, LANES), BF16),
            pltpu.VMEM((2, slab, LANES, LANES), BF16),
            pltpu.VMEM((2, 2, 2 * GROUP * modes, GROUP * LANES), BF16),
            pltpu.VMEM((slab // GROUP, 2, 8, LANES), F32),
        ],
        compiler_params=pltpu.CompilerParams(vmem_limit_bytes=56 * 1024 * 1024),
        name="hyena_block",
    )(tok, table, taps, residues, decays, seeds, cot)


def pack_taps(conv_taps, skip_gain, start, slab):
    taps = lax.dynamic_slice_in_dim(conv_taps.reshape(9, -1), start, slab, 1)
    gain = lax.dynamic_slice_in_dim(skip_gain, start, slab, 0)[None]
    return jnp.broadcast_to(jnp.concatenate([taps, gain])[:, :, None], (10, slab, LANES))


def body(token_ids, embedding, conv_taps, residues, decays, filter_seed, skip_gain, cotangent):
    axes = ("fsdp", "ctx")
    ctx_size = lax.axis_size("ctx")
    count = ctx_size * lax.axis_size("fsdp")
    width = conv_taps.shape[2]
    slab = width // count
    tok_block = token_ids.shape[1]
    rank = lax.axis_index("ctx")
    start = (lax.axis_index("fsdp") * ctx_size + rank) * slab
    tok = lax.all_gather(token_ids, axes, axis=0, tiled=True)
    table = lax.dynamic_slice_in_dim(embedding, rank * slab, slab, 1).T
    taps = pack_taps(conv_taps, skip_gain, start, slab)
    part = [lax.dynamic_slice_in_dim(p, start, slab, 0) for p in (residues, decays, filter_seed)]
    cot = lax.all_to_all(
        cotangent.reshape(width, tok_block), axes, split_axis=0, concat_axis=0, tiled=True
    )
    mixed, grad = run_block(tok, table, taps, *part, cot, ctx_size, ctx_size * tok_block)
    mixer = lax.all_to_all(mixed, axes, split_axis=0, concat_axis=0, tiled=True)
    grad = lax.all_gather(grad, "ctx", axis=0, tiled=True)
    return mixer.reshape(cotangent.shape), grad.T


def solution(mesh):
    placed = (P("fsdp", "ctx"), P(None, "fsdp"), P(), P(), P(), P(), P(), P("fsdp", None, "ctx"))
    return jax.shard_map(
        body,
        mesh=mesh,
        in_specs=placed,
        out_specs=(P("fsdp", None, "ctx"), P(None, "fsdp")),
        check_vma=False,
    )
```

time: 772 us -> 506 us (0.66)
  blocking collectives: 0 us -> 368 us
  other arithmetic: 249 us -> 0.01 us
  matrix products: 170 us -> 0 us
  waiting for transfers between devices: 191 us -> 49.5 us
  local copies, waits for them, and re-layouts: 92 us -> 14.5 us
  Pallas kernels: 0 us -> 47.6 us
  starting transfers between devices: 48.6 us -> 11.7 us
    all_gather x0 -> x1, blocking collectives: none -> 334 us  [body(): tok = lax.all_gather(token_ids, axes, axis=0, tiled=True)]
    dot_general x31 -> x0, matrix products: 170 us -> none  [the longest x3 30.9 us: forward_dft(): jnp.einsum('bckt,tm->bckm', turned_imag, inner_sin, precision=HIGHEST)]
    psum x1 -> x0, waiting for transfers between devices: 144 us -> none  [body(): embed_grad = lax.psum(half_grad, 'ctx')]
    reduce_sum x1 -> x0, other arithmetic: 133 us -> none  [body(): jnp.sum(weight * jnp.exp(-decay_rate * positions.astype(jnp.float32)[None...]
    unnamed x2 -> x0, other arithmetic: 76.8 us -> none
    pallas_call x0 -> x1, Pallas kernels: none -> 47.6 us  [run_block(): pl.pallas_call(functools.partial(block_kernel, chunks, modes, seq_len), o...]
    all_to_all x0 -> x1, blocking collectives: none -> 34.4 us  [body(): mixer = lax.all_to_all(mixed, axes, split_axis=0, concat_axis=0, tiled=True)]
    all_gather x1, waiting for transfers between devices: 16.5 us -> 49.5 us  [body(): grad = lax.all_gather(grad, 'ctx', axis=0, tiled=True)]
  transfers between devices with their start and end apart: 9 -> 2, of which waited for: 4 -> 1; matrix products, arithmetic and copies ran while one was open for 39% -> 1% of each run, Pallas kernels for 0% -> 0%
where the time goes in v1:
time: 506 us
  blocking collectives  368 us (73%)
  waiting for transfers between devices  49.5 us (10%)
  Pallas kernels  47.6 us (9%)
  local copies, waits for them, and re-layouts  14.5 us (3%)
  between operations  14.1 us (3%)
  starting transfers between devices  11.7 us (2%)
    all_gather x1, blocking collectives, body(): tok = lax.all_gather(token_ids, axes, axis=0, tiled=True)  334 us
    all_gather x1, waiting for transfers between devices, body(): grad = lax.all_gather(grad, 'ctx', axis=0, tiled=True)  49.5 us
    pallas_call x1, Pallas kernels, run_block(): pl.pallas_call(functools.partial(block_kernel, chunks, modes, seq_len), o...  47.6 us
    all_to_all x1, blocking collectives, body(): mixer = lax.all_to_all(mixed, axes, split_axis=0, concat_axis=0, tiled=True)  34.4 us
    all_to_all x1, starting transfers between devices, body(): lax.all_to_all(cotangent.reshape(width, tok_block), axes, split_axis=0, c...  11.7 us
    unnamed x12, local copies, waits for them, and re-layouts  11.1 us
  transfers between devices with their start and end apart: 2, of which 1 were waited for; matrix products, arithmetic and copies ran while one was open for 1% of the time, Pallas kernels for 0%

profile of v1, /device:TPU:0, one launch (start us, length us, event | category | flops | bytes accessed | tf_op | source)
XLA Modules:
  0.0 505.7 jit_solution(1259127093549555757)
XLA Ops:
  7.2 0.0 copy-start
  7.2 0.0 copy-start.1
  7.2 0.0 copy-start.2
  7.2 11.7 %all-to-all-start = ((f32[128,32,128]{2,1,0:T(8,128)}), f32[128,32,128]{2,1,0:T(8,128)}, u32[]{:S(2)}, u32[]{:S(2)}) async-start(f32[128,32,128]{2,1,0:T(8,128)} %bitcast.12), calls=%async_computation | async-start | bytes 4194304 | tf_op jit(solution)/shard_map/all_to_all | solution.py:302
  18.9 0.0 all-gather.3.cloned.1.call-start
  18.9 0.8 constant_dynamic-slice_fusion
  19.7 0.7 copy.24.seeds
  20.4 0.8 constant_dynamic-slice_fusion.1
  21.2 0.7 copy.23.decays
  21.9 0.7 copy.22.residues
  22.5 0.0 copy-done
  22.5 0.1 constant_dynamic-slice_fusion.4
  22.6 0.7 copy.21
  23.3 0.0 copy-done.1
  23.3 0.1 reshape.18
  23.4 0.0 copy-done.2
  23.4 333.9 %all-gather = s32[128,1,128]{2,1,0:T(1,128)} all-gather(s32[1,1,128]{2,1,0:T(1,128)S(1)} %bitcast.16), channel_id=1, replica_groups=mesh['fsdp'=2,'ctx'=64] {'fsdp','ctx'}, dimensions={0}, use_global_device_ids=true | all-gather | bytes 66048 | tf_op jit(solution)/shard_map/all_gather | solution.py:298
  357.3 0.8 dynamic-slice_bitcast_fusion
  358.1 0.1 constant_dynamic-slice_fusion.3
  358.2 0.0 all-to-all-done
  358.2 0.8 broadcast_in_dim.10.taps
  359.0 47.6 %hyena_block.1 = (f32[4096,128]{1,0:T(8,128)}, f32[32,512]{1,0:T(8,128)}) custom-call(s32[128,128]{1,0:T(8,128)} %bitcast.14, bf16[32,512]{1,0:T(8,128)(2,1)} %bitcast.15, f32[10,32,128]{2,1,0:T(8,128)} %broadcast_in_dim.10.taps, f32[32,16]{1,0:T(8,128)} %copy.22.residues, f32[32,16]{1,0:T(8,128)} %copy.23.decays, s32[32,16]{1,0:T(8,128)} %copy.24.seeds, ...), custom_call_target="tpu_custom_call" | custom-call | tf_op jit(solution)/shard_map/hyena_block/pallas_call | solution.py:263
  406.6 0.0 all-gather.3.cloned.1.call-update
  406.6 34.4 %all_to_all.20 = f32[128,32,128]{2,1,0:T(8,128)} all-to-all(f32[128,32,128]{2,1,0:T(8,128)} %bitcast.13), channel_id=1, replica_groups=mesh['fsdp'=2,'ctx'=64] {'fsdp','ctx'}, dimensions={0} | all-to-all | bytes 4194304 | tf_op jit(solution)/shard_map/all_to_all | solution.py:306
  441.0 49.5 %all-gather.3.cloned.1.call-done = f32[2048,512]{1,0:T(8,128)} async-done(((f32[32,512]{1,0:T(8,128)}), f32[2048,512]{1,0:T(8,128)}) %all-gather.3.cloned.1.call-update) | async-done | bytes 4194320 | tf_op jit(solution)/shard_map/all_gather | solution.py:307
  490.5 5.3 %copy.20 = f32[512,2048]{1,0:T(8,128)} copy(f32[512,2048]{0,1:T(8,128)} %bitcast.11) | data formatting | bytes 8388608
  495.8 3.0 copy.26
  (1 shorter events, 0.0 us)
Async XLA Ops:
  7.2 15.4 %copy-start = (bf16[512,2048]{1,0:T(8,128)(2,1)S(1)}, bf16[512,2048]{1,0:T(8,128)(2,1)}, u32[]{:S(2)}) copy-start(bf16[512,2048]{1,0:T(8,128)(2,1)} %param.9) | copy-start | bytes 6291460
  7.2 16.2 %copy-start.1 = (f32[3,3,4096]{2,1,0:T(4,128)S(1)}, f32[3,3,4096]{2,1,0:T(4,128)}, u32[]{:S(2)}) copy-start(f32[3,3,4096]{2,1,0:T(4,128)} %param.10) | copy-start | bytes 442372
  7.2 16.2 %copy-start.2 = (s32[1,128]{1,0:T(1,128)S(1)}, s32[1,128]{1,0:T(1,128)}, u32[]{:S(2)}) copy-start(s32[1,128]{1,0:T(1,128)} %param.8) | copy-start | bytes 1540
  7.2 351.0 %all-to-all-start = ((f32[128,32,128]{2,1,0:T(8,128)}), f32[128,32,128]{2,1,0:T(8,128)}, u32[]{:S(2)}, u32[]{:S(2)}) async-start(f32[128,32,128]{2,1,0:T(8,128)} %bitcast.12), calls=%async_computation | async-start | bytes 4194304 | tf_op jit(solution)/shard_map/all_to_all | solution.py:302
  18.9 471.6 %all-gather.3.cloned.1.call-start = ((), (), s32[]{:S(2)}) async-start(), calls=%async_computation.2 | async-start | bytes 4259840 | tf_op jit(solution)/shard_map/all_gather | solution.py:307
Sparse Core Ops, SparseCore 0:
  406.7 83.7 all-gather.2

commit v2 on v1

--- a/solution.py
+++ b/solution.py
@@ -61,18 +61,95 @@
     return both[:rows] + both[rows:] + dot(left_high, right_low)
 
 
+MESH = pl.DeviceIdType.MESH
+
+
 def block_kernel(
-    chunks, modes, seq_len,
-    tok, table, taps, residues, decays, seeds, cot,
-    mixed_out, table_grad,
-    query, key, value, mix, long_out,
+    chunks, seq_len,
+    tok_mine, embedding, conv_taps, gains, residue_all, decay_all, seed_all, cot_mine,
+    mixer, table_grad,
+    query, key, value, mix, long_out, cot, mixed_out,
+    tok, table, taps, residues, decays, seeds, raw_table, turned, raw_taps,
     bank, toeplitz, diag, state_rows,
+    load_sems, tok_sems, cot_sems, mixer_sems,
 ):
     rows = tok.shape[0]
     slab = table.shape[0]
     vocab = table.shape[1]
+    modes = residues.shape[1]
     groups = slab // GROUP
     wide = GROUP * modes
+    ctx = lax.axis_index("ctx")
+    me = lax.axis_index("fsdp") * chunks + ctx
+    per_tile = LANES // slab
+
+    def device(i):
+        peer = lax.rem(me + i, rows)
+        return peer, (peer // chunks, lax.rem(peer, chunks))
+
+    def slab_rows(index):
+        return pl.ds(pl.multiple_of(index * slab, slab), slab)
+
+    barrier = pltpu.get_barrier_semaphore()
+
+    @pl.loop(1, rows)
+    def _(i):
+        pl.semaphore_signal(barrier, inc=1, device_id=device(i)[1], device_id_type=MESH)
+
+    lane_tile = pl.ds(pl.multiple_of(ctx // per_tile * LANES, LANES), LANES)
+    wide_tile = pl.ds(pl.multiple_of(me // per_tile * LANES, LANES), LANES)
+    loads = [
+        pltpu.make_async_copy(source, target, load_sems.at[n])
+        for n, (source, target) in enumerate((
+            (residue_all.at[slab_rows(me)], residues),
+            (decay_all.at[slab_rows(me)], decays),
+            (seed_all.at[slab_rows(me)], seeds),
+            (conv_taps.at[:, :, wide_tile], raw_taps),
+            (embedding.at[:, lane_tile], raw_table),
+        ))
+    ]
+    for load in loads:
+        load.start()
+    pl.semaphore_wait(barrier, rows - 1)
+
+    own_tok = pltpu.make_async_copy(tok_mine, tok.at[pl.ds(me, 1)], tok_sems.at[1])
+    own_tok.start()
+
+    @pl.loop(1, rows)
+    def _(i):
+        pltpu.make_async_remote_copy(
+            src_ref=tok_mine, dst_ref=tok.at[pl.ds(me, 1)],
+            send_sem=tok_sems.at[0], recv_sem=tok_sems.at[1],
+            device_id=device(i)[1], device_id_type=MESH,
+        ).start()
+
+    own_cot = pltpu.make_async_copy(cot_mine.at[slab_rows(me)], cot.at[slab_rows(me)], cot_sems.at[1])
+    own_cot.start()
+
+    @pl.loop(1, rows)
+    def _(i):
+        peer, where = device(i)
+        pltpu.make_async_remote_copy(
+            src_ref=cot_mine.at[slab_rows(peer)], dst_ref=cot.at[slab_rows(me)],
+            send_sem=cot_sems.at[0], recv_sem=cot_sems.at[1],
+            device_id=where, device_id_type=MESH,
+        ).start()
+
+    def wait_bytes(ref, sem):
+        pltpu.make_async_copy(ref, ref, sem).wait()
+
+    for load in loads:
+        load.wait()
+    sub = pl.ds(pl.multiple_of(lax.rem(ctx, per_tile) * slab, slab), slab)
+    turned[...] = raw_table[...].astype(F32).T
+    table[...] = turned[sub, :].astype(BF16)
+    pieces = [raw_taps[s, j : j + 1, :] for s in range(3) for j in range(3)]
+    pieces.append(gains[pl.ds(me // per_tile, 1), :])
+    pieces.append(jnp.zeros((LANES - 10, LANES), F32))
+    turned[:, :LANES] = jnp.concatenate(pieces, axis=0).T
+    columns = turned[sub, :LANES]
+    for j in range(10):
+        taps[j] = jnp.broadcast_to(columns[:, j : j + 1], (slab, LANES))
 
     spread = (iota((slab * modes, slab), 0) // modes == iota((slab * modes, slab), 1)).astype(F32)
     pick = iota((slab * modes, modes), 0) % modes == iota((slab * modes, modes), 1)
@@ -124,6 +201,7 @@
 
     diag[...] = jnp.zeros_like(diag)
 
+    wait_bytes(tok, tok_sems.at[1])
     lane_c = iota((slab, LANES), 1)
     vocab_row = iota((vocab, LANES), 0)
 
@@ -210,14 +288,29 @@
 
     long_conv(mix, long_out, False)
 
-    def emit(r, _):
-        at = pl.ds(pl.multiple_of(r * slab, slab), slab)
-        q = query[at, :]
-        mixed_out[at, :] = q * long_out[at, :]
-        mix[at, :] = cot[at, :] * q
+    def emit(i, _):
+        r, where = device(i)
+        at = slab_rows(r)
+        mixed_out[at, :] = query[at, :] * long_out[at, :]
+        pltpu.make_async_remote_copy(
+            src_ref=mixed_out.at[at], dst_ref=mixer.at[slab_rows(me)],
+            send_sem=mixer_sems.at[0], recv_sem=mixer_sems.at[1],
+            device_id=where, device_id_type=MESH,
+        ).start()
         return 0
 
-    lax.fori_loop(0, rows, emit, 0, unroll=4)
+    mixed_out[slab_rows(me), :] = query[slab_rows(me), :] * long_out[slab_rows(me), :]
+    pltpu.make_async_copy(
+        mixed_out.at[slab_rows(me)], mixer.at[slab_rows(me)], mixer_sems.at[1]
+    ).start()
+    lax.fori_loop(1, rows, emit, 0)
+    wait_bytes(cot, cot_sems.at[1])
+
+    def weigh(r, _):
+        mix[slab_rows(r), :] = cot[slab_rows(r), :] * query[slab_rows(r), :]
+        return 0
+
+    lax.fori_loop(0, rows, weigh, 0, unroll=8)
 
     grad_mixed = query
     long_conv(mix, grad_mixed, True)
@@ -252,60 +345,108 @@
         0, rows // UNROLL, scatter, (zero, zero, jnp.zeros((2 * slab, vocab), F32))
     )
     table_grad[...] = total[:slab] + total[slab:]
-
-
-def run_block(tok, table, taps, residues, decays, seeds, cot, chunks, seq_len):
-    rows = tok.shape[0]
-    slab, vocab = table.shape
-    modes = residues.shape[1]
+    most = pl.ds(0, (rows - 1) * slab)
+    wait_bytes(tok.at[pl.ds(0, rows - 1)], tok_sems.at[0])
+    wait_bytes(cot.at[most], cot_sems.at[0])
+    wait_bytes(mixed_out.at[most], mixer_sems.at[0])
+    wait_bytes(mixer, mixer_sems.at[1])
+
+
+def run_block(tok, embedding, conv_taps, gains, residues, decays, seeds, cot, chunks):
+    width, modes = residues.shape
+    vocab = embedding.shape[0]
+    rows = width // (embedding.shape[1] // chunks)
+    slab = width // rows
     tall = rows * slab
     vmem = pl.BlockSpec(memory_space=pltpu.VMEM)
+    hbm = pl.BlockSpec(memory_space=pl.ANY)
+    dma = pltpu.SemaphoreType.DMA
     return pl.pallas_call(
-        functools.partial(block_kernel, chunks, modes, seq_len),
+        functools.partial(block_kernel, chunks, chunks * LANES),
         out_shape=(
             jax.ShapeDtypeStruct((tall, LANES), F32),
             jax.ShapeDtypeStruct((slab, vocab), F32),
         ),
-        in_specs=[vmem] * 7,
-        out_specs=(vmem, vmem),
-        scratch_shapes=[pltpu.VMEM((tall, LANES), F32)] * 5
+        in_specs=[vmem, hbm, hbm, vmem, hbm, hbm, hbm, hbm],
+        out_specs=(hbm, vmem),
+        scratch_shapes=[pltpu.VMEM((tall, LANES), F32)] * 7
         + [
+            pltpu.VMEM((rows, LANES), jnp.int32),
+            pltpu.VMEM((slab, vocab), BF16),
+            pltpu.VMEM((10, slab, LANES), F32),
+            pltpu.VMEM((slab, modes), F32),
+            pltpu.VMEM((slab, modes), F32),
+            pltpu.VMEM((slab, modes), jnp.int32),
+            pltpu.VMEM((vocab, LANES), BF16),
+            pltpu.VMEM((LANES, vocab), F32),
+            pltpu.VMEM((3, 3, LANES), F32),
             pltpu.VMEM((8, slab * modes, LANES), BF16),
             pltpu.VMEM((2, slab, LANES, LANES), BF16),
             pltpu.VMEM((2, 2, 2 * GROUP * modes, GROUP * LANES), BF16),
             pltpu.VMEM((slab // GROUP, 2, 8, LANES), F32),
+            dma((5,)), dma((2,)), dma((2,)), dma((2,)),
         ],
-        compiler_params=pltpu.CompilerParams(vmem_limit_bytes=56 * 1024 * 1024),
+        compiler_params=pltpu.CompilerParams(
+            vmem_limit_bytes=56 * 1024 * 1024, collective_id=0, has_side_effects=True
+        ),
         name="hyena_block",
-    )(tok, table, taps, residues, decays, seeds, cot)
-
-
-def pack_taps(conv_taps, skip_gain, start, slab):
-    taps = lax.dynamic_slice_in_dim(conv_taps.reshape(9, -1), start, slab, 1)
-    gain = lax.dynamic_slice_in_dim(skip_gain, start, slab, 0)[None]
-    return jnp.broadcast_to(jnp.concatenate([taps, gain])[:, :, None], (10, slab, LANES))
+    )(tok, embedding, conv_taps, gains, residues, decays, seeds, cot)
+
+
+def spread_kernel(sides, mine, every, own_sem, sems):
+    chunks = every.shape[0]
+    ctx = lax.axis_index("ctx")
+    fsdp = lax.axis_index("fsdp")
+    barrier = pltpu.get_barrier_semaphore()
+
+    def peer(i):
+        return (fsdp, lax.rem(ctx + i, chunks))
+
+    @pl.loop(1, chunks)
+    def _(i):
+        pl.semaphore_signal(barrier, inc=1, device_id=peer(i), device_id_type=MESH)
+
+    own = pltpu.make_async_copy(mine, every.at[ctx], own_sem)
+    own.start()
+    pl.semaphore_wait(barrier, chunks - 1)
+
+    @pl.loop(1, chunks)
+    def _(i):
+        pltpu.make_async_remote_copy(
+            src_ref=mine, dst_ref=every.at[ctx],
+            send_sem=sems.at[0], recv_sem=sems.at[1],
+            device_id=peer(i), device_id_type=MESH,
+        ).start()
+
+    own.wait()
+    most = every.at[pl.ds(0, chunks - 1)]
+    pltpu.make_async_copy(most, most, sems.at[0]).wait()
+    pltpu.make_async_copy(most, most, sems.at[1]).wait()
+
+
+def spread(block, chunks):
+    hbm = pl.BlockSpec(memory_space=pl.ANY)
+    return pl.pallas_call(
+        functools.partial(spread_kernel, None),
+        out_shape=jax.ShapeDtypeStruct((chunks, *block.shape), block.dtype),
+        in_specs=[pl.BlockSpec(memory_space=pltpu.VMEM)],
+        out_specs=hbm,
+        scratch_shapes=[pltpu.SemaphoreType.DMA, pltpu.SemaphoreType.DMA((2,))],
+        compiler_params=pltpu.CompilerParams(collective_id=1, has_side_effects=True),
+        name="grad_spread",
+    )(block)
 
 
 def body(token_ids, embedding, conv_taps, residues, decays, filter_seed, skip_gain, cotangent):
-    axes = ("fsdp", "ctx")
     ctx_size = lax.axis_size("ctx")
-    count = ctx_size * lax.axis_size("fsdp")
     width = conv_taps.shape[2]
-    slab = width // count
     tok_block = token_ids.shape[1]
-    rank = lax.axis_index("ctx")
-    start = (lax.axis_index("fsdp") * ctx_size + rank) * slab
-    tok = lax.all_gather(token_ids, axes, axis=0, tiled=True)
-    table = lax.dynamic_slice_in_dim(embedding, rank * slab, slab, 1).T
-    taps = pack_taps(conv_taps, skip_gain, start, slab)
-    part = [lax.dynamic_slice_in_dim(p, start, slab, 0) for p in (residues, decays, filter_seed)]
-    cot = lax.all_to_all(
-        cotangent.reshape(width, tok_block), axes, split_axis=0, concat_axis=0, tiled=True
+    mixer, grad = run_block(
+        token_ids, embedding, conv_taps, skip_gain.reshape(-1, LANES),
+        residues, decays, filter_seed, cotangent.reshape(width, tok_block), ctx_size,
     )
-    mixed, grad = run_block(tok, table, taps, *part, cot, ctx_size, ctx_size * tok_block)
-    mixer = lax.all_to_all(mixed, axes, split_axis=0, concat_axis=0, tiled=True)
-    grad = lax.all_gather(grad, "ctx", axis=0, tiled=True)
-    return mixer.reshape(cotangent.shape), grad.T
+    grad = spread(grad, ctx_size)
+    return mixer.reshape(cotangent.shape), grad.reshape(-1, grad.shape[2]).T
 
 
 def solution(mesh):

time: 506 us -> 160 us (0.32)
  the two profiles are of different devices: /device:TPU:0 before, /device:TPU:70 now
where the time goes in v2:
time: 160 us
  Pallas kernels  146 us (91%)
  local copies, waits for them, and re-layouts  13.6 us (8%)
    pallas_call x1, Pallas kernels, spread(): pl.pallas_call(functools.partial(spread_kernel, None), out_shape=jax.Shap...  79.7 us
    pallas_call x1, Pallas kernels, run_block(): pl.pallas_call(functools.partial(block_kernel, chunks, chunks * LANES), o...  65.9 us
    unnamed x10, local copies, waits for them, and re-layouts  8.14 us
    reshape x1, local copies, waits for them, and re-layouts, body(): return (mixer.reshape(cotangent.shape), grad.reshape(-1, grad.shape[2]).T)  5.49 us

profile of v2, /device:TPU:70, one launch (start us, length us, event | category | flops | bytes accessed | tf_op | source)
XLA Modules:
  0.0 159.9 jit_solution(12008830437683613342)
XLA Ops:
  0.6 0.0 copy-start.1
  0.6 0.0 copy-start.2
  0.7 2.9 %copy.10.residue_all = f32[4096,16]{1,0:T(8,128)} copy(f32[4096,16]{0,1:T(8,128)} %param.11) | data formatting | bytes 524288 | tf_op args[3]
  3.6 0.0 copy-done.1
  3.6 1.9 %copy.11.decay_all = f32[4096,16]{1,0:T(8,128)} copy(f32[4096,16]{0,1:T(8,128)S(1)} %copy-done.1) | data formatting | bytes 524288 | tf_op args[4]
  5.5 0.0 copy-done.2
  5.5 1.9 %copy.12.seed_all = s32[4096,16]{1,0:T(8,128)} copy(s32[4096,16]{0,1:T(8,128)S(1)} %copy-done.2) | data formatting | bytes 524288 | tf_op args[5]
  7.5 65.9 %hyena_block.1 = (f32[4096,128]{1,0:T(8,128)}, f32[32,512]{1,0:T(8,128)}) custom-call(s32[1,128]{1,0:T(1,128)} %tok_mine.1, bf16[512,2048]{1,0:T(8,128)(2,1)} %embedding.1, f32[3,3,4096]{2,1,0:T(4,128)} %conv_taps.1, f32[32,128]{1,0:T(8,128)} %bitcast.9, f32[4096,16]{1,0:T(8,128)} %copy.10.residue_all, f32[4096,16]{1,0:T(8,128)} %copy.11.decay_all, ...), custom_call_target="tpu_custom_call" | custom-call | tf_op jit(solution)/shard_map/hyena_block/pallas_call | solution.py:364
  73.4 79.7 %grad_spread.1 = f32[64,32,512]{2,1,0:T(8,128)} custom-call(f32[32,512]{1,0:T(8,128)} %get-tuple-element.5.mine), custom_call_target="tpu_custom_call" | custom-call | tf_op jit(solution)/shard_map/grad_spread/pallas_call | solution.py:429
  153.1 0.0 copy-start
  153.1 5.5 %copy.13 = f32[2048,512]{0,1:T(8,128)} copy(f32[2048,512]{1,0:T(8,128)} %bitcast.5) | data formatting | bytes 8388608 | tf_op jit(solution)/shard_map/reshape | solution.py:449
  158.6 0.0 copy-done
  158.6 1.3 copy.15
Async XLA Ops:
  0.6 3.0 %copy-start.1 = (f32[4096,16]{0,1:T(8,128)S(1)}, f32[4096,16]{0,1:T(8,128)}, u32[]{:S(2)}) copy-start(f32[4096,16]{0,1:T(8,128)} %param.12) | copy-start | bytes 786436
  0.6 4.9 %copy-start.2 = (s32[4096,16]{0,1:T(8,128)S(1)}, s32[4096,16]{0,1:T(8,128)}, u32[]{:S(2)}) copy-start(s32[4096,16]{0,1:T(8,128)} %param.13) | copy-start | bytes 786436
  153.1 5.5 %copy-start = (f32[4096,128]{1,0:T(8,128)S(1)}, f32[4096,128]{1,0:T(8,128)}, u32[]{:S(2)}) copy-start(f32[4096,128]{1,0:T(8,128)} %get-tuple-element.4) | copy-start | bytes 6291460

commit v3 on v2

--- a/solution.py
+++ b/solution.py
@@ -76,7 +76,7 @@
     rows = tok.shape[0]
     slab = table.shape[0]
     vocab = table.shape[1]
-    modes = residues.shape[1]
+    modes = residues.shape[0]
     groups = slab // GROUP
     wide = GROUP * modes
     ctx = lax.axis_index("ctx")
@@ -101,9 +101,9 @@
     loads = [
         pltpu.make_async_copy(source, target, load_sems.at[n])
         for n, (source, target) in enumerate((
-            (residue_all.at[slab_rows(me)], residues),
-            (decay_all.at[slab_rows(me)], decays),
-            (seed_all.at[slab_rows(me)], seeds),
+            (residue_all.at[:, wide_tile], residues),
+            (decay_all.at[:, wide_tile], decays),
+            (seed_all.at[:, wide_tile], seeds),
             (conv_taps.at[:, :, wide_tile], raw_taps),
             (embedding.at[:, lane_tile], raw_table),
         ))
@@ -143,13 +143,14 @@
     sub = pl.ds(pl.multiple_of(lax.rem(ctx, per_tile) * slab, slab), slab)
     turned[...] = raw_table[...].astype(F32).T
     table[...] = turned[sub, :].astype(BF16)
-    pieces = [raw_taps[s, j : j + 1, :] for s in range(3) for j in range(3)]
+    pieces = [residues[...], decays[...], seeds[...].astype(F32)]
+    pieces += [raw_taps[s, j : j + 1, :] for s in range(3) for j in range(3)]
     pieces.append(gains[pl.ds(me // per_tile, 1), :])
-    pieces.append(jnp.zeros((LANES - 10, LANES), F32))
+    pieces.append(jnp.zeros((LANES - 10 - 3 * modes, LANES), F32))
     turned[:, :LANES] = jnp.concatenate(pieces, axis=0).T
     columns = turned[sub, :LANES]
     for j in range(10):
-        taps[j] = jnp.broadcast_to(columns[:, j : j + 1], (slab, LANES))
+        taps[j] = jnp.broadcast_to(columns[:, 3 * modes + j : 3 * modes + j + 1], (slab, LANES))
 
     spread = (iota((slab * modes, slab), 0) // modes == iota((slab * modes, slab), 1)).astype(F32)
     pick = iota((slab * modes, modes), 0) % modes == iota((slab * modes, modes), 1)
@@ -158,9 +159,9 @@
         wide_part = jnp.dot(spread, part, precision=lax.Precision.HIGHEST, preferred_element_type=F32)
         return jnp.sum(jnp.where(pick, wide_part, 0.0), axis=1, keepdims=True)
 
-    rate = column(decays[...])
-    seed = column(seeds[...].astype(F32))
-    res = column(residues[...])
+    rate = column(columns[:, modes : 2 * modes])
+    seed = column(columns[:, 2 * modes : 3 * modes])
+    res = column(columns[:, :modes])
     weight = res * jnp.sqrt(rate + 1.0 / seq_len)
     seed_int = (seed + 0.5).astype(jnp.int32)
     rate_b = jnp.broadcast_to(rate, (slab * modes, LANES))
@@ -344,7 +345,10 @@
     _, _, total = lax.fori_loop(
         0, rows // UNROLL, scatter, (zero, zero, jnp.zeros((2 * slab, vocab), F32))
     )
-    table_grad[...] = total[:slab] + total[slab:]
+    total = total[:slab] + total[slab:]
+    for i in range(slab // 8):
+        for j in range(vocab // LANES):
+            table_grad[i * (vocab // LANES) + j] = total[i * 8 : (i + 1) * 8, j * LANES : (j + 1) * LANES]
     most = pl.ds(0, (rows - 1) * slab)
     wait_bytes(tok.at[pl.ds(0, rows - 1)], tok_sems.at[0])
     wait_bytes(cot.at[most], cot_sems.at[0])
@@ -353,7 +357,7 @@
 
 
 def run_block(tok, embedding, conv_taps, gains, residues, decays, seeds, cot, chunks):
-    width, modes = residues.shape
+    modes, width = residues.shape
     vocab = embedding.shape[0]
     rows = width // (embedding.shape[1] // chunks)
     slab = width // rows
@@ -365,7 +369,7 @@
         functools.partial(block_kernel, chunks, chunks * LANES),
         out_shape=(
             jax.ShapeDtypeStruct((tall, LANES), F32),
-            jax.ShapeDtypeStruct((slab, vocab), F32),
+            jax.ShapeDtypeStruct((slab * vocab // (8 * LANES), 8, LANES), F32),
         ),
         in_specs=[vmem, hbm, hbm, vmem, hbm, hbm, hbm, hbm],
         out_specs=(hbm, vmem),
@@ -374,9 +378,9 @@
             pltpu.VMEM((rows, LANES), jnp.int32),
             pltpu.VMEM((slab, vocab), BF16),
             pltpu.VMEM((10, slab, LANES), F32),
-            pltpu.VMEM((slab, modes), F32),
-            pltpu.VMEM((slab, modes), F32),
-            pltpu.VMEM((slab, modes), jnp.int32),
+            pltpu.VMEM((modes, LANES), F32),
+            pltpu.VMEM((modes, LANES), F32),
+            pltpu.VMEM((modes, LANES), jnp.int32),
             pltpu.VMEM((vocab, LANES), BF16),
             pltpu.VMEM((LANES, vocab), F32),
             pltpu.VMEM((3, 3, LANES), F32),
@@ -393,48 +397,120 @@
     )(tok, embedding, conv_taps, gains, residues, decays, seeds, cot)
 
 
-def spread_kernel(sides, mine, every, own_sem, sems):
-    chunks = every.shape[0]
+AXES = ("z", "x", "y")
+
+
+def spread_kernel(sides, parts, mine, every, own_sem, send_sems, recv_sems):
     ctx = lax.axis_index("ctx")
     fsdp = lax.axis_index("fsdp")
+    spans = (sides[1] * sides[2], sides[2], 1)
+    here = [lax.rem(ctx // span, side) for span, side in zip(spans, sides)]
+
+    def device(axis, hop):
+        there = lax.rem(here[axis] + hop + sides[axis], sides[axis])
+        return (fsdp, ctx + (there - here[axis]) * spans[axis])
+
+    def at(axis, hop, done, first, size):
+        index = []
+        for n in range(3):
+            if n == axis:
+                index.append(pl.ds(lax.rem(here[n] + hop + sides[n], sides[n]), 1))
+            elif n in done:
+                index.append(slice(None))
+            else:
+                index.append(pl.ds(here[n], 1))
+        return every.at[(*index, pl.ds(first, size))]
+
     barrier = pltpu.get_barrier_semaphore()
-
-    def peer(i):
-        return (fsdp, lax.rem(ctx + i, chunks))
-
-    @pl.loop(1, chunks)
-    def _(i):
-        pl.semaphore_signal(barrier, inc=1, device_id=peer(i), device_id_type=MESH)
-
-    own = pltpu.make_async_copy(mine, every.at[ctx], own_sem)
+    for axis in range(3):
+        for hop in (1, -1, 2):
+            pl.semaphore_signal(barrier, inc=1, device_id=device(axis, hop), device_id_type=MESH)
+    own = pltpu.make_async_copy(mine, every.at[here[0], here[1], here[2]], own_sem)
     own.start()
-    pl.semaphore_wait(barrier, chunks - 1)
-
-    @pl.loop(1, chunks)
-    def _(i):
-        pltpu.make_async_remote_copy(
-            src_ref=mine, dst_ref=every.at[ctx],
-            send_sem=sems.at[0], recv_sem=sems.at[1],
-            device_id=peer(i), device_id_type=MESH,
-        ).start()
-
+    pl.semaphore_wait(barrier, 9)
     own.wait()
-    most = every.at[pl.ds(0, chunks - 1)]
-    pltpu.make_async_copy(most, most, sems.at[0]).wait()
-    pltpu.make_async_copy(most, most, sems.at[1]).wait()
+
+    sent = []
+
+    def copy(part, phase, slot, source, where):
+        made = pltpu.make_async_remote_copy(
+            src_ref=source, dst_ref=source,
+            send_sem=send_sems.at[part, phase, slot], recv_sem=recv_sems.at[part, phase, slot],
+            device_id=where, device_id_type=MESH,
+        )
+        made.start()
+        sent.append(made)
+
+    def landed(part, phase, slot, place):
+        pltpu.make_async_copy(place, place, recv_sems.at[part, phase, slot]).wait()
+
+    for phase in range(3):
+        plan = []
+        for part, (first, size) in enumerate(parts):
+            order = [(2 - part + n) % 3 for n in range(3)]
+            axis, done = order[phase], order[:phase]
+            plan.append((part, axis, done, first, size))
+            block = at(axis, 0, done, first, size)
+            copy(part, phase, 0, block, device(axis, 1))
+            copy(part, phase, 1, block, device(axis, -1))
+            if phase < 2:
+                copy(part, phase, 2, block, device(axis, 2))
+        for part, axis, done, first, size in plan:
+            half = size // 2
+            landed(part, phase, 0, at(axis, -1, done, first, size))
+            if phase == 2:
+                copy(part, phase, 2, at(axis, -1, done, first, half), device(axis, 1))
+            landed(part, phase, 1, at(axis, 1, done, first, size))
+            if phase == 2:
+                copy(part, phase, 3, at(axis, 1, done, first + half, size - half), device(axis, -1))
+        for part, axis, done, first, size in plan:
+            half = size // 2
+            if phase < 2:
+                landed(part, phase, 2, at(axis, 2, done, first, size))
+            else:
+                landed(part, phase, 2, at(axis, 2, done, first, half))
+                landed(part, phase, 3, at(axis, 2, done, first + half, size - half))
+    for made in sent:
+        made.wait_send()
 
 
 def spread(block, chunks):
-    hbm = pl.BlockSpec(memory_space=pl.ANY)
+    side = round(chunks ** (1 / 3))
+    tiles = block.shape[0]
+    third = tiles // 3
+    parts = ((0, third), (third, third), (2 * third, tiles - 2 * third))
+    dma = pltpu.SemaphoreType.DMA
     return pl.pallas_call(
-        functools.partial(spread_kernel, None),
-        out_shape=jax.ShapeDtypeStruct((chunks, *block.shape), block.dtype),
+        functools.partial(spread_kernel, (side,) * 3, parts),
+        out_shape=jax.ShapeDtypeStruct((side,) * 3 + block.shape, block.dtype),
         in_specs=[pl.BlockSpec(memory_space=pltpu.VMEM)],
-        out_specs=hbm,
-        scratch_shapes=[pltpu.SemaphoreType.DMA, pltpu.SemaphoreType.DMA((2,))],
+        out_specs=pl.BlockSpec(memory_space=pltpu.VMEM),
+        scratch_shapes=[dma, dma((3, 3, 4)), dma((3, 3, 4))],
         compiler_params=pltpu.CompilerParams(collective_id=1, has_side_effects=True),
         name="grad_spread",
     )(block)
+
+
+def turn_kernel(tiles, out):
+    per, count = tiles.shape[0], tiles.shape[1]
+    across = out.shape[0] // LANES
+    for j in range(across):
+        rows = [tiles[s, i * across + j] for s in range(per) for i in range(count // across)]
+        out[j * LANES : (j + 1) * LANES, :] = jnp.concatenate(rows, axis=0).T
+
+
+def turn(every, vocab):
+    sources, tiles = math.prod(every.shape[:3]), every.shape[3]
+    slab = tiles * 8 * LANES // vocab
+    per = LANES // slab
+    return pl.pallas_call(
+        turn_kernel,
+        grid=(sources // per,),
+        out_shape=jax.ShapeDtypeStruct((vocab, sources * slab), every.dtype),
+        in_specs=[pl.BlockSpec((per, tiles, 8, LANES), lambda n: (n, 0, 0, 0))],
+        out_specs=pl.BlockSpec((vocab, LANES), lambda n: (0, n)),
+        name="grad_turn",
+    )(every.reshape(sources, tiles, 8, LANES))
 
 
 def body(token_ids, embedding, conv_taps, residues, decays, filter_seed, skip_gain, cotangent):
@@ -443,10 +519,10 @@
     tok_block = token_ids.shape[1]
     mixer, grad = run_block(
         token_ids, embedding, conv_taps, skip_gain.reshape(-1, LANES),
-        residues, decays, filter_seed, cotangent.reshape(width, tok_block), ctx_size,
+        residues.T, decays.T, filter_seed.T, cotangent.reshape(width, tok_block), ctx_size,
     )
-    grad = spread(grad, ctx_size)
-    return mixer.reshape(cotangent.shape), grad.reshape(-1, grad.shape[2]).T
+    grad = turn(spread(grad, ctx_size), embedding.shape[0])
+    return mixer.reshape(cotangent.shape), grad
 
 
 def solution(mesh):

time: 160 us -> 113 us (0.71)
  the two profiles are of different devices: /device:TPU:70 before, /device:TPU:0 now
where the time goes in v3:
time: 113 us; the launch traced here: 112 us
  Pallas kernels  110 us (97%)
  local copies, waits for them, and re-layouts  1.32 us (1%)
    pallas_call x1, Pallas kernels, run_block(): pl.pallas_call(functools.partial(block_kernel, chunks, chunks * LANES), o...  69.5 us
    pallas_call x1, Pallas kernels, spread(): pl.pallas_call(functools.partial(spread_kernel, (side,) * 3, parts), out_...  29.6 us
    pallas_call x1, Pallas kernels, turn(): pl.pallas_call(turn_kernel, grid=(sources // per,), out_shape=jax.ShapeDt...  11 us

profile of v3, /device:TPU:0, one launch (start us, length us, event | category | flops | bytes accessed | tf_op | source)
XLA Modules:
  0.0 112.1 jit_solution(3361659008399129245)
XLA Ops:
  0.6 69.5 %hyena_block.1 = (f32[4096,128]{1,0:T(8,128)}, f32[16,8,128]{2,1,0:T(8,128)}) custom-call(s32[1,128]{1,0:T(1,128)} %tok_mine.1, bf16[512,2048]{1,0:T(8,128)(2,1)} %embedding.1, f32[3,3,4096]{2,1,0:T(4,128)} %conv_taps.1, f32[32,128]{1,0:T(8,128)} %bitcast.13, f32[16,4096]{1,0:T(8,128)} %bitcast.10, f32[16,4096]{1,0:T(8,128)} %bitcast.11, ...), custom_call_target="tpu_custom_call" | custom-call | tf_op jit(solution)/shard_map/hyena_block/pallas_call | solution.py:368
  70.2 29.6 %grad_spread.1 = f32[4,4,4,16,8,128]{5,4,3,2,1,0:T(8,128)} custom-call(f32[16,8,128]{2,1,0:T(8,128)} %get-tuple-element.5.mine), custom_call_target="tpu_custom_call" | custom-call | tf_op jit(solution)/shard_map/grad_spread/pallas_call | solution.py:483
  99.8 0.0 copy-start
  99.8 11.0 %grad_turn.1 = f32[512,2048]{1,0:T(8,128)} custom-call(f32[64,16,8,128]{3,2,1,0:T(8,128)} %bitcast.7), custom_call_target="tpu_custom_call" | custom-call | tf_op jit(solution)/shard_map/grad_turn/pallas_call | solution.py:506
  110.8 0.0 copy-done
  110.8 1.3 %copy.11 = f32[1,4096,128]{2,1,0:T(8,128)} copy(f32[1,4096,128]{2,1,0:T(8,128)S(1)} %bitcast.8) | data formatting | bytes 4194304
Async XLA Ops:
  99.8 11.0 %copy-start = (f32[4096,128]{1,0:T(8,128)S(1)}, f32[4096,128]{1,0:T(8,128)}, u32[]{:S(2)}) copy-start(f32[4096,128]{1,0:T(8,128)} %get-tuple-element.4) | copy-start | bytes 6291460

commit v4 on v2

--- a/solution.py
+++ b/solution.py
@@ -64,19 +64,120 @@
 MESH = pl.DeviceIdType.MESH
 
 
+LEVELS = 32767.0
+
+
+def gather_grad(total, chunks, quarters, columns_of, every, scales, turn_sems, send_sems, recv_sems):
+    sides = every.shape[:3]
+    ctx = lax.axis_index("ctx")
+    fsdp = lax.axis_index("fsdp")
+    spans = (sides[1] * sides[2], sides[2], 1)
+    here = [lax.rem(ctx // span, side) for span, side in zip(spans, sides)]
+    slab = total.shape[0]
+    sent = []
+
+    def neighbour(axis, hop):
+        there = lax.rem(here[axis] + hop + sides[axis], sides[axis])
+        return there, (fsdp, ctx + (there - here[axis]) * spans[axis])
+
+    def send(source, target, sender, receiver, where):
+        made = pltpu.make_async_remote_copy(
+            src_ref=source, dst_ref=target, send_sem=sender, recv_sem=receiver,
+            device_id=where, device_id_type=MESH,
+        )
+        made.start()
+        sent.append(made)
+
+    def landed(place, sem):
+        pltpu.make_async_copy(place, place, sem).wait()
+
+    for j in range(sides[2]):
+        quarters[j] = total[:, j * LANES : (j + 1) * LANES]
+    strip = pl.ds(pl.multiple_of(here[2] * slab, slab), slab)
+    for n, hop in enumerate((1, -1, 2)):
+        there, where = neighbour(2, hop)
+        send(quarters.at[there], columns_of.at[strip], turn_sems.at[0, n], turn_sems.at[1, n], where)
+    columns_of[strip, :] = quarters[here[2]]
+    for n, hop in enumerate((-1, 1, 2)):
+        there = neighbour(2, hop)[0]
+        landed(columns_of.at[pl.ds(pl.multiple_of(there * slab, slab), slab)], turn_sems.at[1, n])
+    block = columns_of[...].T
+    peak = jnp.max(jnp.abs(block), axis=0, keepdims=True)
+    block = jnp.round(block * (LEVELS / jnp.maximum(peak, 1e-30))).astype(jnp.int32).astype(jnp.int16)
+    tiles = every.shape[3]
+    every[here[0], here[1], here[2]] = block.reshape(tiles, LANES // tiles, LANES)
+    scales[here[0], here[1], here[2]] = peak * (1.0 / LEVELS)
+
+    def at(ref, axis, hop, done, *rest):
+        index = []
+        for n in range(3):
+            if n == axis:
+                index.append(pl.ds(lax.rem(here[n] + hop + sides[n], sides[n]), 1))
+            elif n in done:
+                index.append(slice(None))
+            else:
+                index.append(pl.ds(here[n], 1))
+        return ref.at[(*index, *rest)]
+
+    third = -(-tiles // 3)
+    cuts = (0, third, 2 * third, tiles)
+    for phase in range(3):
+        plan = []
+        for part in range(3):
+            order = [(2 - part + n) % 3 for n in range(3)]
+            axis, done = order[phase], order[:phase]
+            first, size = cuts[part], cuts[part + 1] - cuts[part]
+            half = size // 2
+            whole, low, high = pl.ds(first, size), pl.ds(first, half), pl.ds(first + half, size - half)
+            plan.append((part, axis, done, whole, low, high))
+            right, left = neighbour(axis, 1)[1], neighbour(axis, -1)[1]
+            mine = at(every, axis, 0, done, whole)
+            sems = (send_sems.at[part, phase], recv_sems.at[part, phase])
+            send(mine, mine, sems[0].at[0], sems[1].at[0], right)
+            send(mine, mine, sems[0].at[1], sems[1].at[1], left)
+            if phase < 2:
+                send(mine, mine, sems[0].at[2], sems[1].at[2], neighbour(axis, 2)[1])
+            if part == 2:
+                level = at(scales, axis, 0, done)
+                for n, hop in enumerate((1, -1, 2)):
+                    send(level, level, sems[0].at[4 + n], sems[1].at[4 + n], neighbour(axis, hop)[1])
+        for part, axis, done, whole, low, high in plan:
+            sems = (send_sems.at[part, phase], recv_sems.at[part, phase])
+            landed(at(every, axis, -1, done, whole), sems[1].at[0])
+            if phase == 2:
+                piece = at(every, axis, -1, done, low)
+                send(piece, piece, sems[0].at[2], sems[1].at[2], neighbour(axis, 1)[1])
+            landed(at(every, axis, 1, done, whole), sems[1].at[1])
+            if phase == 2:
+                piece = at(every, axis, 1, done, high)
+                send(piece, piece, sems[0].at[3], sems[1].at[3], neighbour(axis, -1)[1])
+        for part, axis, done, whole, low, high in plan:
+            sem = recv_sems.at[part, phase]
+            if phase < 2:
+                landed(at(every, axis, 2, done, whole), sem.at[2])
+            else:
+                landed(at(every, axis, 2, done, low), sem.at[2])
+                landed(at(every, axis, 2, done, high), sem.at[3])
+            if part == 2:
+                for n, hop in enumerate((-1, 1, 2)):
+                    landed(at(scales, axis, hop, done), sem.at[4 + n])
+    for made in sent:
+        made.wait_send()
+
+
 def block_kernel(
     chunks, seq_len,
     tok_mine, embedding, conv_taps, gains, residue_all, decay_all, seed_all, cot_mine,
-    mixer, table_grad,
+    mixer, every, scales,
     query, key, value, mix, long_out, cot, mixed_out,
     tok, table, taps, residues, decays, seeds, raw_table, turned, raw_taps,
-    bank, toeplitz, diag, state_rows,
-    load_sems, tok_sems, cot_sems, mixer_sems,
+    bank, toeplitz, diag, state_rows, quarters, columns_of,
+    load_sems, tok_sems, cot_sems, mixer_sems, turn_sems, send_sems, recv_sems,
 ):
     rows = tok.shape[0]
     slab = table.shape[0]
     vocab = table.shape[1]
-    modes = residues.shape[1]
+    modes = residues.shape[0]
     groups = slab // GROUP
     wide = GROUP * modes
     ctx = lax.axis_index("ctx")
@@ -101,9 +202,9 @@
     loads = [
         pltpu.make_async_copy(source, target, load_sems.at[n])
         for n, (source, target) in enumerate((
-            (residue_all.at[slab_rows(me)], residues),
-            (decay_all.at[slab_rows(me)], decays),
-            (seed_all.at[slab_rows(me)], seeds),
+            (residue_all.at[:, wide_tile], residues),
+            (decay_all.at[:, wide_tile], decays),
+            (seed_all.at[:, wide_tile], seeds),
             (conv_taps.at[:, :, wide_tile], raw_taps),
             (embedding.at[:, lane_tile], raw_table),
         ))
@@ -143,13 +244,14 @@
     sub = pl.ds(pl.multiple_of(lax.rem(ctx, per_tile) * slab, slab), slab)
     turned[...] = raw_table[...].astype(F32).T
     table[...] = turned[sub, :].astype(BF16)
-    pieces = [raw_taps[s, j : j + 1, :] for s in range(3) for j in range(3)]
+    pieces = [residues[...], decays[...], seeds[...].astype(F32)]
+    pieces += [raw_taps[s, j : j + 1, :] for s in range(3) for j in range(3)]
     pieces.append(gains[pl.ds(me // per_tile, 1), :])
-    pieces.append(jnp.zeros((LANES - 10, LANES), F32))
+    pieces.append(jnp.zeros((LANES - 10 - 3 * modes, LANES), F32))
     turned[:, :LANES] = jnp.concatenate(pieces, axis=0).T
     columns = turned[sub, :LANES]
     for j in range(10):
-        taps[j] = jnp.broadcast_to(columns[:, j : j + 1], (slab, LANES))
+        taps[j] = jnp.broadcast_to(columns[:, 3 * modes + j : 3 * modes + j + 1], (slab, LANES))
 
     spread = (iota((slab * modes, slab), 0) // modes == iota((slab * modes, slab), 1)).astype(F32)
     pick = iota((slab * modes, modes), 0) % modes == iota((slab * modes, modes), 1)
@@ -158,9 +260,9 @@
         wide_part = jnp.dot(spread, part, precision=lax.Precision.HIGHEST, preferred_element_type=F32)
         return jnp.sum(jnp.where(pick, wide_part, 0.0), axis=1, keepdims=True)
 
-    rate = column(decays[...])
-    seed = column(seeds[...].astype(F32))
-    res = column(residues[...])
+    rate = column(columns[:, modes : 2 * modes])
+    seed = column(columns[:, 2 * modes : 3 * modes])
+    res = column(columns[:, :modes])
     weight = res * jnp.sqrt(rate + 1.0 / seq_len)
     seed_int = (seed + 0.5).astype(jnp.int32)
     rate_b = jnp.broadcast_to(rate, (slab * modes, LANES))
@@ -344,7 +446,10 @@
     _, _, total = lax.fori_loop(
         0, rows // UNROLL, scatter, (zero, zero, jnp.zeros((2 * slab, vocab), F32))
     )
-    table_grad[...] = total[:slab] + total[slab:]
+    gather_grad(
+        total[:slab] + total[slab:], chunks, quarters, columns_of, every, scales,
+        turn_sems, send_sems, recv_sems,
+    )
     most = pl.ds(0, (rows - 1) * slab)
     wait_bytes(tok.at[pl.ds(0, rows - 1)], tok_sems.at[0])
     wait_bytes(cot.at[most], cot_sems.at[0])
@@ -353,11 +458,12 @@
 
 
 def run_block(tok, embedding, conv_taps, gains, residues, decays, seeds, cot, chunks):
-    width, modes = residues.shape
+    modes, width = residues.shape
     vocab = embedding.shape[0]
     rows = width // (embedding.shape[1] // chunks)
     slab = width // rows
     tall = rows * slab
+    side = round(chunks ** (1 / 3))
     vmem = pl.BlockSpec(memory_space=pltpu.VMEM)
     hbm = pl.BlockSpec(memory_space=pl.ANY)
     dma = pltpu.SemaphoreType.DMA
@@ -365,18 +471,19 @@
         functools.partial(block_kernel, chunks, chunks * LANES),
         out_shape=(
             jax.ShapeDtypeStruct((tall, LANES), F32),
-            jax.ShapeDtypeStruct((slab, vocab), F32),
+            jax.ShapeDtypeStruct((side,) * 3 + (8, LANES // 8, LANES), jnp.int16),
+            jax.ShapeDtypeStruct((side,) * 3 + (1, LANES), F32),
         ),
         in_specs=[vmem, hbm, hbm, vmem, hbm, hbm, hbm, hbm],
-        out_specs=(hbm, vmem),
+        out_specs=(hbm, vmem, vmem),
         scratch_shapes=[pltpu.VMEM((tall, LANES), F32)] * 7
         + [
             pltpu.VMEM((rows, LANES), jnp.int32),
             pltpu.VMEM((slab, vocab), BF16),
             pltpu.VMEM((10, slab, LANES), F32),
-            pltpu.VMEM((slab, modes), F32),
-            pltpu.VMEM((slab, modes), F32),
-            pltpu.VMEM((slab, modes), jnp.int32),
+            pltpu.VMEM((modes, LANES), F32),
+            pltpu.VMEM((modes, LANES), F32),
+            pltpu.VMEM((modes, LANES), jnp.int32),
             pltpu.VMEM((vocab, LANES), BF16),
             pltpu.VMEM((LANES, vocab), F32),
             pltpu.VMEM((3, 3, LANES), F32),
@@ -384,7 +491,9 @@
             pltpu.VMEM((2, slab, LANES, LANES), BF16),
             pltpu.VMEM((2, 2, 2 * GROUP * modes, GROUP * LANES), BF16),
             pltpu.VMEM((slab // GROUP, 2, 8, LANES), F32),
-            dma((5,)), dma((2,)), dma((2,)), dma((2,)),
+            pltpu.VMEM((side, slab, LANES), F32),
+            pltpu.VMEM((LANES, LANES), F32),
+            dma((5,)), dma((2,)), dma((2,)), dma((2,)), dma((2, 3)), dma((3, 3, 7)), dma((3, 3, 7)),
         ],
         compiler_params=pltpu.CompilerParams(
             vmem_limit_bytes=56 * 1024 * 1024, collective_id=0, has_side_effects=True
@@ -393,60 +502,38 @@
     )(tok, embedding, conv_taps, gains, residues, decays, seeds, cot)
 
 
-def spread_kernel(sides, mine, every, own_sem, sems):
-    chunks = every.shape[0]
-    ctx = lax.axis_index("ctx")
-    fsdp = lax.axis_index("fsdp")
-    barrier = pltpu.get_barrier_semaphore()
-
-    def peer(i):
-        return (fsdp, lax.rem(ctx + i, chunks))
-
-    @pl.loop(1, chunks)
-    def _(i):
-        pl.semaphore_signal(barrier, inc=1, device_id=peer(i), device_id_type=MESH)
-
-    own = pltpu.make_async_copy(mine, every.at[ctx], own_sem)
-    own.start()
-    pl.semaphore_wait(barrier, chunks - 1)
-
-    @pl.loop(1, chunks)
-    def _(i):
-        pltpu.make_async_remote_copy(
-            src_ref=mine, dst_ref=every.at[ctx],
-            send_sem=sems.at[0], recv_sem=sems.at[1],
-            device_id=peer(i), device_id_type=MESH,
-        ).start()
-
-    own.wait()
-    most = every.at[pl.ds(0, chunks - 1)]
-    pltpu.make_async_copy(most, most, sems.at[0]).wait()
-    pltpu.make_async_copy(most, most, sems.at[1]).wait()
-
-
-def spread(block, chunks):
-    hbm = pl.BlockSpec(memory_space=pl.ANY)
+def finish_kernel(every, scales, out):
+    for z in range(every.shape[0]):
+        for x in range(every.shape[1]):
+            n = z * every.shape[1] + x
+            values = every[z, x, 0].reshape(LANES, LANES).astype(jnp.int32).astype(F32)
+            out[:, n * LANES : (n + 1) * LANES] = values * scales[z, x, 0]
+
+
+def finish(every, scales):
+    a, b, c, tiles = every.shape[:4]
     return pl.pallas_call(
-        functools.partial(spread_kernel, None),
-        out_shape=jax.ShapeDtypeStruct((chunks, *block.shape), block.dtype),
-        in_specs=[pl.BlockSpec(memory_space=pltpu.VMEM)],
-        out_specs=hbm,
-        scratch_shapes=[pltpu.SemaphoreType.DMA, pltpu.SemaphoreType.DMA((2,))],
-        compiler_params=pltpu.CompilerParams(collective_id=1, has_side_effects=True),
-        name="grad_spread",
-    )(block)
+        finish_kernel,
+        grid=(c,),
+        out_shape=jax.ShapeDtypeStruct((c * LANES, a * b * LANES), F32),
+        in_specs=[
+            pl.BlockSpec((a, b, 1, *every.shape[3:]), lambda n: (0, 0, n, 0, 0, 0)),
+            pl.BlockSpec((a, b, 1, 1, LANES), lambda n: (0, 0, n, 0, 0)),
+        ],
+        out_specs=pl.BlockSpec((LANES, a * b * LANES), lambda n: (n, 0)),
+        name="grad_finish",
+    )(every, scales)
 
 
 def body(token_ids, embedding, conv_taps, residues, decays, filter_seed, skip_gain, cotangent):
     ctx_size = lax.axis_size("ctx")
     width = conv_taps.shape[2]
     tok_block = token_ids.shape[1]
-    mixer, grad = run_block(
+    mixer, every, scales = run_block(
         token_ids, embedding, conv_taps, skip_gain.reshape(-1, LANES),
-        residues, decays, filter_seed, cotangent.reshape(width, tok_block), ctx_size,
+        residues.T, decays.T, filter_seed.T, cotangent.reshape(width, tok_block), ctx_size,
     )
-    grad = spread(grad, ctx_size)
-    return mixer.reshape(cotangent.shape), grad.reshape(-1, grad.shape[2]).T
+    return mixer.reshape(cotangent.shape), finish(every, scales)
 
 
 def solution(mesh):

time: 160 us -> 96.4 us (0.60)
  the two profiles are of different devices: /device:TPU:70 before, /device:TPU:0 now
where the time goes in v4:
time: 96.4 us; the launch traced here: 96.1 us
  Pallas kernels  94.2 us (98%)
  local copies, waits for them, and re-layouts  1.32 us (1%)
    pallas_call x1, Pallas kernels, run_block(): pl.pallas_call(functools.partial(block_kernel, chunks, chunks * LANES), o...  89.7 us
    pallas_call x1, Pallas kernels, finish(): pl.pallas_call(finish_kernel, grid=(c,), out_shape=jax.ShapeDtypeStruct((...  4.49 us

profile of v4, /device:TPU:0, one launch (start us, length us, event | category | flops | bytes accessed | tf_op | source)
XLA Modules:
  0.0 96.1 jit_solution(9640983702639983389)
XLA Ops:
  0.6 89.7 %hyena_block.1 = (f32[4096,128]{1,0:T(8,128)}, s16[4,4,4,8,16,128]{5,4,3,2,1,0:T(8,128)(2,1)}, f32[4,4,4,1,128]{4,3,2,1,0:T(1,128)}) custom-call(s32[1,128]{1,0:T(1,128)} %tok_mine.1, bf16[512,2048]{1,0:T(8,128)(2,1)} %embedding.1, f32[3,3,4096]{2,1,0:T(4,128)} %conv_taps.1, f32[32,128]{1,0:T(8,128)} %bitcast.11, f32[16,4096]{1,0:T(8,128)} %bitcast.8, ...), custom_call_target="tpu_custom_call" | custom-call | tf_op jit(solution)/shard_map/hyena_block/pallas_call | solution.py:470
  90.3 0.0 copy-start
  90.3 4.5 %grad_finish.1 = f32[512,2048]{1,0:T(8,128)} custom-call(s16[4,4,4,8,16,128]{5,4,3,2,1,0:T(8,128)(2,1)} %get-tuple-element.6.every, f32[4,4,4,1,128]{4,3,2,1,0:T(1,128)} %get-tuple-element.7.scales), custom_call_target="tpu_custom_call" | custom-call | tf_op jit(solution)/shard_map/grad_finish/pallas_call | solution.py:515
  94.8 0.0 copy-done
  94.8 1.3 %copy.11 = f32[1,4096,128]{2,1,0:T(8,128)} copy(f32[1,4096,128]{2,1,0:T(8,128)S(1)} %bitcast.6) | data formatting | bytes 4194304
Async XLA Ops:
  90.3 4.5 %copy-start = (f32[4096,128]{1,0:T(8,128)S(1)}, f32[4096,128]{1,0:T(8,128)}, u32[]{:S(2)}) copy-start(f32[4096,128]{1,0:T(8,128)} %get-tuple-element.5) | copy-start | bytes 6291460

commit v5 on v4

--- a/solution.py
+++ b/solution.py
@@ -67,13 +67,13 @@
 LEVELS = 32767.0
 
 
-def gather_grad(total, chunks, quarters, columns_of, every, scales, turn_sems, send_sems, recv_sems):
+def gather_grad(pieces, chunks, quarters, columns_of, every, scales, turn_sems, send_sems, recv_sems):
     sides = every.shape[:3]
     ctx = lax.axis_index("ctx")
     fsdp = lax.axis_index("fsdp")
     spans = (sides[1] * sides[2], sides[2], 1)
     here = [lax.rem(ctx // span, side) for span, side in zip(spans, sides)]
-    slab = total.shape[0]
+    slab = pieces[0].shape[0]
     sent = []
 
     def neighbour(axis, hop):
@@ -92,7 +92,7 @@
         pltpu.make_async_copy(place, place, sem).wait()
 
     for j in range(sides[2]):
-        quarters[j] = total[:, j * LANES : (j + 1) * LANES]
+        quarters[j] = pieces[j]
     strip = pl.ds(pl.multiple_of(here[2] * slab, slab), slab)
     for n, hop in enumerate((1, -1, 2)):
         there, where = neighbour(2, hop)
@@ -168,34 +168,51 @@
 def block_kernel(
     chunks, seq_len,
     tok_mine, embedding, conv_taps, gains, residue_all, decay_all, seed_all, cot_mine,
-    mixer, every, scales,
-    query, key, value, mix, long_out, cot, mixed_out,
-    tok, table, taps, residues, decays, seeds, raw_table, turned, raw_taps,
+    mixer, mixer_scale, every, scales,
+    query, key, value, mix, long_out, cot, cot_out, cot_in, mixed_out, level_out, head_out, head_in,
+    staged, table, taps, residues, decays, seeds, raw_table, turned, raw_taps,
     bank, toeplitz, diag, state_rows, quarters, columns_of,
-    load_sems, tok_sems, cot_sems, mixer_sems, turn_sems, send_sems, recv_sems,
+    load_sems, head_sems, cot_sems, mixer_sems, level_sems, turn_sems, send_sems, recv_sems,
 ):
-    rows = tok.shape[0]
-    slab = table.shape[0]
-    vocab = table.shape[1]
+    vocab = embedding.shape[0]
+    rows = head_in.shape[0] // 2
+    slab = cot.shape[0] // rows
     modes = residues.shape[0]
     groups = slab // GROUP
     wide = GROUP * modes
     ctx = lax.axis_index("ctx")
-    me = lax.axis_index("fsdp") * chunks + ctx
+    fsdp = lax.axis_index("fsdp")
+    me = fsdp * chunks + ctx
     per_tile = LANES // slab
-
-    def device(i):
-        peer = lax.rem(me + i, rows)
-        return peer, (peer // chunks, lax.rem(peer, chunks))
 
     def slab_rows(index):
         return pl.ds(pl.multiple_of(index * slab, slab), slab)
 
+    def pair(index):
+        return pl.ds(pl.multiple_of(2 * index, 2), 2)
+
+    def each_peer(action):
+        action((1 - fsdp) * chunks + ctx, (1 - fsdp, ctx))
+
+        def step(i, _):
+            there = ctx + i
+            there = jnp.where(there >= chunks, there - chunks, there)
+            for side in (fsdp, 1 - fsdp):
+                action(side * chunks + there, (side, there))
+            return 0
+
+        lax.fori_loop(1, chunks, step, 0, unroll=7)
+
+    def send(source, target, sems, where):
+        pltpu.make_async_remote_copy(
+            src_ref=source, dst_ref=target, send_sem=sems.at[0], recv_sem=sems.at[1],
+            device_id=where, device_id_type=MESH,
+        ).start()
+
     barrier = pltpu.get_barrier_semaphore()
-
-    @pl.loop(1, rows)
-    def _(i):
-        pl.semaphore_signal(barrier, inc=1, device_id=device(i)[1], device_id_type=MESH)
+    load_cot = pltpu.make_async_copy(cot_mine, cot, load_sems.at[5])
+    load_cot.start()
+    each_peer(lambda place, where: pl.semaphore_signal(barrier, inc=1, device_id=where, device_id_type=MESH))
 
     lane_tile = pl.ds(pl.multiple_of(ctx // per_tile * LANES, LANES), LANES)
     wide_tile = pl.ds(pl.multiple_of(me // per_tile * LANES, LANES), LANES)
@@ -211,30 +228,34 @@
     ]
     for load in loads:
         load.start()
+
+    def fixed(block):
+        peak = jnp.maximum(jnp.max(jnp.abs(block), axis=0, keepdims=True), 1e-30)
+        code = jnp.round(block * (LEVELS / peak)).astype(jnp.int32).astype(jnp.int16)
+        return code, peak * (1.0 / LEVELS)
+
+    def real(code, level):
+        return code.astype(jnp.int32).astype(F32) * level
+
+    load_cot.wait()
+    tokens = tok_mine[...].astype(F32)
+
+    def encode(step, _):
+        heads = []
+        for i in range(16):
+            r = step * 16 + i
+            code, level = fixed(cot[slab_rows(r), :])
+            cot_out[slab_rows(r), :] = code
+            heads += [tokens, level]
+        head_out[pl.ds(pl.multiple_of(step * 32, 32), 32), :] = jnp.concatenate(heads, axis=0)
+        return 0
+
+    lax.fori_loop(0, rows // 16, encode, 0)
     pl.semaphore_wait(barrier, rows - 1)
-
-    own_tok = pltpu.make_async_copy(tok_mine, tok.at[pl.ds(me, 1)], tok_sems.at[1])
-    own_tok.start()
-
-    @pl.loop(1, rows)
-    def _(i):
-        pltpu.make_async_remote_copy(
-            src_ref=tok_mine, dst_ref=tok.at[pl.ds(me, 1)],
-            send_sem=tok_sems.at[0], recv_sem=tok_sems.at[1],
-            device_id=device(i)[1], device_id_type=MESH,
-        ).start()
-
-    own_cot = pltpu.make_async_copy(cot_mine.at[slab_rows(me)], cot.at[slab_rows(me)], cot_sems.at[1])
-    own_cot.start()
-
-    @pl.loop(1, rows)
-    def _(i):
-        peer, where = device(i)
-        pltpu.make_async_remote_copy(
-            src_ref=cot_mine.at[slab_rows(peer)], dst_ref=cot.at[slab_rows(me)],
-            send_sem=cot_sems.at[0], recv_sem=cot_sems.at[1],
-            device_id=where, device_id_type=MESH,
-        ).start()
+    each_peer(lambda place, where: send(head_out.at[pair(place)], head_in.at[pair(me)], head_sems, where))
+    each_peer(lambda place, where: send(cot_out.at[slab_rows(place)], cot_in.at[slab_rows(me)], cot_sems, where))
+    head_in[pair(me), :] = head_out[pair(me), :]
+    cot_in[slab_rows(me), :] = cot_out[slab_rows(me), :]
 
     def wait_bytes(ref, sem):
         pltpu.make_async_copy(ref, ref, sem).wait()
@@ -243,7 +264,8 @@
         load.wait()
     sub = pl.ds(pl.multiple_of(lax.rem(ctx, per_tile) * slab, slab), slab)
     turned[...] = raw_table[...].astype(F32).T
-    table[...] = turned[sub, :].astype(BF16)
+    for b in range(vocab // LANES):
+        table[b * slab : (b + 1) * slab, :] = turned[sub, b * LANES : (b + 1) * LANES].astype(BF16)
     pieces = [residues[...], decays[...], seeds[...].astype(F32)]
     pieces += [raw_taps[s, j : j + 1, :] for s in range(3) for j in range(3)]
     pieces.append(gains[pl.ds(me // per_tile, 1), :])
@@ -303,25 +325,32 @@
 
     diag[...] = jnp.zeros_like(diag)
 
-    wait_bytes(tok, tok_sems.at[1])
+    wait_bytes(head_in.at[pl.ds(0, 2 * (rows - 1))], head_sems.at[1])
     lane_c = iota((slab, LANES), 1)
-    vocab_row = iota((vocab, LANES), 0)
-
-    def one_hot(r):
-        return jnp.where(vocab_row == tok[pl.ds(r, 1), :], 1.0, 0.0).astype(BF16)
-
-    UNROLL = 4
+    low_row = iota((LANES, LANES), 0)
+    banks = vocab // LANES
+
+    def token_parts(r):
+        token = (head_in[pl.ds(2 * r, 1), :] + 0.5).astype(jnp.int32)
+        bank_of = token // LANES
+        hot = jnp.where(low_row == token - bank_of * LANES, 1.0, 0.0).astype(BF16)
+        return hot, bank_of
+
+    UNROLL = 16
 
     def gather(step, carry):
         last_one, last_two = carry
         r0 = step * UNROLL
-        hot = jnp.concatenate([one_hot(r0 + i) for i in range(UNROLL)], axis=1)
-        found = nn(table[...], hot)
+        parts = [token_parts(r0 + i) for i in range(UNROLL)]
+        found = nn(table[...], jnp.concatenate([hot for hot, _ in parts], axis=1))
         fresh = (r0 % chunks) == 0
         last_one = jnp.where(fresh, 0.0, last_one)
         last_two = jnp.where(fresh, 0.0, last_two)
         for i in range(UNROLL):
-            x = found[:, i * LANES : (i + 1) * LANES]
+            bank_of = parts[i][1]
+            x = found[:slab, i * LANES : (i + 1) * LANES]
+            for b in range(1, banks):
+                x = jnp.where(bank_of == b, found[b * slab : (b + 1) * slab, i * LANES : (i + 1) * LANES], x)
             one = pltpu.roll(x, 1, 1)
             two = pltpu.roll(x, 2, 1)
             x1 = jnp.where(lane_c < 1, last_one, one)
@@ -361,58 +390,62 @@
 
         def per_group(g, _):
             base = g * GROUP
-            for side, first in enumerate((enter, leave)):
-                for c in range(GROUP):
-                    at = pl.ds(pl.multiple_of(g * wide + c * modes, modes), modes)
-                    for half in range(2):
-                        spot = slice(half * wide + c * modes, half * wide + (c + 1) * modes)
-                        for part in range(2):
-                            diag[side, part, spot, c * LANES : (c + 1) * LANES] = bank[
-                                2 * (first + half) + part, at, :
-                            ]
+            for c in range(GROUP):
+                at = pl.ds(pl.multiple_of(g * wide + c * modes, modes), modes)
+                for half in range(2):
+                    spot = slice(half * wide + c * modes, half * wide + (c + 1) * modes)
+                    for part in range(2):
+                        diag[part, spot, c * LANES : (c + 1) * LANES] = bank[2 * (enter + half) + part, at, :]
             local = jnp.zeros((rows, 2 * wide), F32)
             for c in range(GROUP):
                 u = split(source[pl.ds(base + c, rows, stride=slab), :])
+                staged[0, base + c], staged[1, base + c] = u
                 at = slice(c * LANES, (c + 1) * LANES)
-                local = local + three(nt, u, (diag[0, 0, :, at], diag[0, 1, :, at]))
+                local = local + three(nt, u, (diag[0, :, at], diag[1, :, at]))
             re, im = scan(local[:, :wide], local[:, wide:], g, backward)
             state = split(jnp.concatenate([re, im], axis=1))
             for c in range(GROUP):
-                u = split(source[pl.ds(base + c, rows, stride=slab), :])
+                u = (staged[0, base + c], staged[1, base + c])
                 at = slice(c * LANES, (c + 1) * LANES)
                 band = (toeplitz[0, base + c], toeplitz[1, base + c])
                 out = three(nt if backward else nn, u, band)
-                out = out + three(nn, state, (diag[1, 0, :, at], diag[1, 1, :, at]))
+                mine = slice(c * modes, (c + 1) * modes)
+                held = [jnp.concatenate([p[:, mine], p[:, wide + c * modes : wide + (c + 1) * modes]], axis=1) for p in state]
+                rows_at = pl.ds(pl.multiple_of(g * wide + c * modes, modes), modes)
+                pole = [
+                    jnp.concatenate([bank[2 * leave + part, rows_at, :], bank[2 * (leave + 1) + part, rows_at, :]], axis=0)
+                    for part in range(2)
+                ]
+                out = out + three(nn, held, pole)
                 target[pl.ds(base + c, rows, stride=slab), :] = out
             return 0
 
-        lax.fori_loop(0, groups, per_group, 0)
+        lax.fori_loop(0, groups, per_group, 0, unroll=2)
 
     long_conv(mix, long_out, False)
 
-    def emit(i, _):
-        r, where = device(i)
-        at = slab_rows(r)
-        mixed_out[at, :] = query[at, :] * long_out[at, :]
-        pltpu.make_async_remote_copy(
-            src_ref=mixed_out.at[at], dst_ref=mixer.at[slab_rows(me)],
-            send_sem=mixer_sems.at[0], recv_sem=mixer_sems.at[1],
-            device_id=where, device_id_type=MESH,
-        ).start()
+    def emit(place, where):
+        at = slab_rows(place)
+        mixed_out[at, :], level_out[place] = fixed(query[at, :] * long_out[at, :])
+        send(mixed_out.at[at], mixer.at[slab_rows(me)], mixer_sems, where)
+        send(level_out.at[place], mixer_scale.at[me], level_sems, where)
+
+    each_peer(emit)
+    at = slab_rows(me)
+    mixer[at, :], mixer_scale[me] = fixed(query[at, :] * long_out[at, :])
+    most = pl.ds(0, (rows - 1) * slab)
+    wait_bytes(cot_in.at[most], cot_sems.at[1])
+
+    def weigh(step, _):
+        for i in range(8):
+            r = step * 8 + i
+            at = slab_rows(r)
+            value_in = real(cot_in[at, :], head_in[pl.ds(2 * r + 1, 1), :])
+            cot[at, :] = value_in
+            mix[at, :] = value_in * query[at, :]
         return 0
 
-    mixed_out[slab_rows(me), :] = query[slab_rows(me), :] * long_out[slab_rows(me), :]
-    pltpu.make_async_copy(
-        mixed_out.at[slab_rows(me)], mixer.at[slab_rows(me)], mixer_sems.at[1]
-    ).start()
-    lax.fori_loop(1, rows, emit, 0)
-    wait_bytes(cot, cot_sems.at[1])
-
-    def weigh(r, _):
-        mix[slab_rows(r), :] = cot[slab_rows(r), :] * query[slab_rows(r), :]
-        return 0
-
-    lax.fori_loop(0, rows, weigh, 0, unroll=8)
+    lax.fori_loop(0, rows // 8, weigh, 0)
 
     grad_mixed = query
     long_conv(mix, grad_mixed, True)
@@ -423,7 +456,7 @@
         fresh = (r0 % chunks) == chunks - UNROLL
         next_one = jnp.where(fresh, 0.0, next_one)
         next_two = jnp.where(fresh, 0.0, next_two)
-        pieces = [None] * UNROLL
+        pieces, hots = [None] * UNROLL, [None] * UNROLL
         for i in reversed(range(UNROLL)):
             at = pl.ds(pl.multiple_of((r0 + i) * slab, slab), slab)
             gm = grad_mixed[at, :]
@@ -439,22 +472,26 @@
                 + jnp.where(lane_c >= LANES - 2, next_two, two)
             )
             next_one, next_two = one, two
-            pieces[i] = jnp.concatenate(split(gx), axis=0)
-        hot = jnp.concatenate([one_hot(r0 + i) for i in range(UNROLL)], axis=1)
+            hots[i], bank_of = token_parts(r0 + i)
+            both = jnp.concatenate(split(gx), axis=0)
+            mask = [jnp.where(bank_of == b, 1.0, 0.0).astype(BF16) for b in range(banks)]
+            pieces[i] = jnp.concatenate([both * m for m in mask], axis=0)
+        hot = jnp.concatenate(hots, axis=1)
         return next_one, next_two, total + nt(jnp.concatenate(pieces, axis=1), hot)
 
     _, _, total = lax.fori_loop(
-        0, rows // UNROLL, scatter, (zero, zero, jnp.zeros((2 * slab, vocab), F32))
+        0, rows // UNROLL, scatter, (zero, zero, jnp.zeros((2 * slab * banks, LANES), F32))
     )
+    step = 2 * slab
+    pieces = [total[b * step : b * step + slab] + total[b * step + slab : (b + 1) * step] for b in range(banks)]
     gather_grad(
-        total[:slab] + total[slab:], chunks, quarters, columns_of, every, scales,
-        turn_sems, send_sems, recv_sems,
+        pieces, chunks, quarters, columns_of, every, scales, turn_sems, send_sems, recv_sems
     )
-    most = pl.ds(0, (rows - 1) * slab)
-    wait_bytes(tok.at[pl.ds(0, rows - 1)], tok_sems.at[0])
-    wait_bytes(cot.at[most], cot_sems.at[0])
-    wait_bytes(mixed_out.at[most], mixer_sems.at[0])
-    wait_bytes(mixer, mixer_sems.at[1])
+    wait_bytes(head_in.at[pl.ds(0, 2 * (rows - 1))], head_sems.at[0])
+    wait_bytes(cot_in.at[most], cot_sems.at[0])
+    for end in range(2):
+        wait_bytes(mixer.at[most], mixer_sems.at[end])
+        wait_bytes(mixer_scale.at[pl.ds(0, rows - 1)], level_sems.at[end])
 
 
 def run_block(tok, embedding, conv_taps, gains, residues, decays, seeds, cot, chunks):
@@ -470,16 +507,21 @@
     return pl.pallas_call(
         functools.partial(block_kernel, chunks, chunks * LANES),
         out_shape=(
-            jax.ShapeDtypeStruct((tall, LANES), F32),
+            jax.ShapeDtypeStruct((tall, LANES), jnp.int16),
+            jax.ShapeDtypeStruct((rows, 1, LANES), F32),
             jax.ShapeDtypeStruct((side,) * 3 + (8, LANES // 8, LANES), jnp.int16),
             jax.ShapeDtypeStruct((side,) * 3 + (1, LANES), F32),
         ),
         in_specs=[vmem, hbm, hbm, vmem, hbm, hbm, hbm, hbm],
-        out_specs=(hbm, vmem, vmem),
-        scratch_shapes=[pltpu.VMEM((tall, LANES), F32)] * 7
+        out_specs=(vmem, vmem, vmem, vmem),
+        scratch_shapes=[pltpu.VMEM((tall, LANES), F32)] * 6
+        + [pltpu.VMEM((tall, LANES), jnp.int16)] * 3
         + [
-            pltpu.VMEM((rows, LANES), jnp.int32),
-            pltpu.VMEM((slab, vocab), BF16),
+            pltpu.VMEM((rows, 1, LANES), F32),
+            pltpu.VMEM((2 * rows, LANES), F32),
+            pltpu.VMEM((2 * rows, LANES), F32),
+            pltpu.VMEM((2, slab, LANES, LANES), BF16),
+            pltpu.VMEM((vocab // LANES * slab, LANES), BF16),
             pltpu.VMEM((10, slab, LANES), F32),
             pltpu.VMEM((modes, LANES), F32),
             pltpu.VMEM((modes, LANES), F32),
@@ -489,11 +531,11 @@
             pltpu.VMEM((3, 3, LANES), F32),
             pltpu.VMEM((8, slab * modes, LANES), BF16),
             pltpu.VMEM((2, slab, LANES, LANES), BF16),
-            pltpu.VMEM((2, 2, 2 * GROUP * modes, GROUP * LANES), BF16),
+            pltpu.VMEM((2, 2 * GROUP * modes, GROUP * LANES), BF16),
             pltpu.VMEM((slab // GROUP, 2, 8, LANES), F32),
             pltpu.VMEM((side, slab, LANES), F32),
             pltpu.VMEM((LANES, LANES), F32),
-            dma((5,)), dma((2,)), dma((2,)), dma((2,)), dma((2, 3)), dma((3, 3, 7)), dma((3, 3, 7)),
+            dma((6,)), dma((2,)), dma((2,)), dma((2,)), dma((2,)), dma((2, 3)), dma((3, 3, 7)), dma((3, 3, 7)),
         ],
         compiler_params=pltpu.CompilerParams(
             vmem_limit_bytes=56 * 1024 * 1024, collective_id=0, has_side_effects=True
@@ -502,38 +544,53 @@
     )(tok, embedding, conv_taps, gains, residues, decays, seeds, cot)
 
 
-def finish_kernel(every, scales, out):
+def finish_kernel(every, scales, mixer, mixer_scale, grad_out, mixer_out):
     for z in range(every.shape[0]):
         for x in range(every.shape[1]):
             n = z * every.shape[1] + x
             values = every[z, x, 0].reshape(LANES, LANES).astype(jnp.int32).astype(F32)
-            out[:, n * LANES : (n + 1) * LANES] = values * scales[z, x, 0]
-
-
-def finish(every, scales):
+            grad_out[:, n * LANES : (n + 1) * LANES] = values * scales[z, x, 0]
+    count = mixer_scale.shape[0]
+    slab = mixer.shape[0] // count
+    for n in range(count):
+        at = slice(n * slab, (n + 1) * slab)
+        mixer_out[at, :] = mixer[at, :].astype(jnp.int32).astype(F32) * mixer_scale[n]
+
+
+def finish(mixer, mixer_scale, every, scales):
     a, b, c, tiles = every.shape[:4]
+    tall, blocks = mixer.shape[0], mixer_scale.shape[0]
     return pl.pallas_call(
         finish_kernel,
         grid=(c,),
-        out_shape=jax.ShapeDtypeStruct((c * LANES, a * b * LANES), F32),
+        out_shape=(
+            jax.ShapeDtypeStruct((c * LANES, a * b * LANES), F32),
+            jax.ShapeDtypeStruct(mixer.shape, F32),
+        ),
         in_specs=[
             pl.BlockSpec((a, b, 1, *every.shape[3:]), lambda n: (0, 0, n, 0, 0, 0)),
             pl.BlockSpec((a, b, 1, 1, LANES), lambda n: (0, 0, n, 0, 0)),
+            pl.BlockSpec((tall // c, LANES), lambda n: (n, 0)),
+            pl.BlockSpec((blocks // c, 1, LANES), lambda n: (n, 0, 0)),
         ],
-        out_specs=pl.BlockSpec((LANES, a * b * LANES), lambda n: (n, 0)),
-        name="grad_finish",
-    )(every, scales)
+        out_specs=(
+            pl.BlockSpec((LANES, a * b * LANES), lambda n: (n, 0)),
+            pl.BlockSpec((tall // c, LANES), lambda n: (n, 0)),
+        ),
+        name="finish",
+    )(every, scales, mixer, mixer_scale)
 
 
 def body(token_ids, embedding, conv_taps, residues, decays, filter_seed, skip_gain, cotangent):
     ctx_size = lax.axis_size("ctx")
     width = conv_taps.shape[2]
     tok_block = token_ids.shape[1]
-    mixer, every, scales = run_block(
+    packed = run_block(
         token_ids, embedding, conv_taps, skip_gain.reshape(-1, LANES),
         residues.T, decays.T, filter_seed.T, cotangent.reshape(width, tok_block), ctx_size,
     )
-    return mixer.reshape(cotangent.shape), finish(every, scales)
+    grad, mixer = finish(*packed)
+    return mixer.reshape(cotangent.shape), grad
 
 
 def solution(mesh):

time: 96.4 us -> 78.7 us (0.82)
  Pallas kernels: 94.2 us -> 77.5 us
  local copies, waits for them, and re-layouts: 1.32 us -> 0 us
    pallas_call x1, Pallas kernels: 89.7 us -> 72.3 us  [run_block(): pl.pallas_call(functools.partial(block_kernel, chunks, chunks * LANES), o...]
    unnamed x3 -> x0, local copies, waits for them, and re-layouts: 1.32 us -> none
where the time goes in v5:
time: 78.7 us; the launch traced here: 78.1 us
  Pallas kernels  77.5 us (98%)
    pallas_call x1, Pallas kernels, run_block(): pl.pallas_call(functools.partial(block_kernel, chunks, chunks * LANES), o...  72.3 us
    pallas_call x1, Pallas kernels, finish(): pl.pallas_call(finish_kernel, grid=(c,), out_shape=(jax.ShapeDtypeStruct(...  5.14 us

profile of v5, /device:TPU:0, one launch (start us, length us, event | category | flops | bytes accessed | tf_op | source)
XLA Modules:
  0.0 78.1 jit_solution(5458313418147746783)
XLA Ops:
  0.6 72.3 %hyena_block.1 = (s16[4096,128]{1,0:T(8,128)(2,1)}, f32[128,1,128]{2,1,0:T(1,128)}, s16[4,4,4,8,16,128]{5,4,3,2,1,0:T(8,128)(2,1)}, f32[4,4,4,1,128]{4,3,2,1,0:T(1,128)}) custom-call(s32[1,128]{1,0:T(1,128)} %tok_mine.1, bf16[512,2048]{1,0:T(8,128)(2,1)} %embedding.1, f32[3,3,4096]{2,1,0:T(4,128)} %conv_taps.1, f32[32,128]{1,0:T(8,128)} %bitcast.10, ...), custom_call_target="tpu_custom_call" | custom-call | tf_op jit(solution)/shard_map/hyena_block/pallas_call | solution.py:507
  73.0 5.1 %finish.1 = (f32[512,2048]{1,0:T(8,128)}, f32[4096,128]{1,0:T(8,128)}) custom-call(s16[4,4,4,8,16,128]{5,4,3,2,1,0:T(8,128)(2,1)} %get-tuple-element.8.every, f32[4,4,4,1,128]{4,3,2,1,0:T(1,128)} %get-tuple-element.9.scales, s16[4096,128]{1,0:T(8,128)(2,1)} %get-tuple-element.10.mixer, f32[128,1,128]{2,1,0:T(1,128)} %get-tuple-element.11.mixer_scale), custom_call_target="tpu_custom_call" | custom-call | tf_op jit(solution)/shard_map/finish/pallas_call | solution.py:563

commit v6 on v5

--- a/solution.py
+++ b/solution.py
@@ -168,14 +168,14 @@
 def block_kernel(
     chunks, seq_len,
     tok_mine, embedding, conv_taps, gains, residue_all, decay_all, seed_all, cot_mine,
-    mixer, mixer_scale, every, scales,
-    query, key, value, mix, long_out, cot, cot_out, cot_in, mixed_out, level_out, head_out, head_in,
+    mixer, every, scales,
+    query, key, value, mix, long_out, cot, cot_out, cot_in, mixed_out, tok,
     staged, table, taps, residues, decays, seeds, raw_table, turned, raw_taps,
     bank, toeplitz, diag, state_rows, quarters, columns_of,
-    load_sems, head_sems, cot_sems, mixer_sems, level_sems, turn_sems, send_sems, recv_sems,
+    load_sems, tok_sems, cot_sems, mixer_sems, turn_sems, send_sems, recv_sems,
 ):
     vocab = embedding.shape[0]
-    rows = head_in.shape[0] // 2
+    rows = tok.shape[0]
     slab = cot.shape[0] // rows
     modes = residues.shape[0]
     groups = slab // GROUP
@@ -187,9 +187,6 @@
 
     def slab_rows(index):
         return pl.ds(pl.multiple_of(index * slab, slab), slab)
-
-    def pair(index):
-        return pl.ds(pl.multiple_of(2 * index, 2), 2)
 
     def each_peer(action):
         action((1 - fsdp) * chunks + ctx, (1 - fsdp, ctx))
@@ -229,33 +226,66 @@
     for load in loads:
         load.start()
 
-    def fixed(block):
+    sent_rows = pl.ds(0, slab + 2)
+
+    def encode(target, place, block):
         peak = jnp.maximum(jnp.max(jnp.abs(block), axis=0, keepdims=True), 1e-30)
-        code = jnp.round(block * (LEVELS / peak)).astype(jnp.int32).astype(jnp.int16)
-        return code, peak * (1.0 / LEVELS)
-
-    def real(code, level):
-        return code.astype(jnp.int32).astype(F32) * level
-
+        power_of = jnp.ceil(jnp.log2(peak * (1.0 / LEVELS)))
+        code = jnp.clip(jnp.round(block * jnp.exp2(-power_of)), -LEVELS, LEVELS)
+        target[place, :slab, :] = code.astype(jnp.int32).astype(jnp.int16)
+        exponent = jnp.broadcast_to(power_of, (16, LANES)).astype(jnp.int32).astype(jnp.int16)
+        target[place, slab:, :] = exponent
+
+    side = round(chunks ** (1 / 3))
+    here = (ctx // (side * side), lax.rem(ctx // side, side), lax.rem(ctx, side))
+    spans = (side * side, side, 1)
+
+    def exchange(phase):
+        axis = 2 - phase
+        if axis < 0:
+            other = (1 - fsdp, ctx)
+            base = pl.ds(pl.multiple_of(fsdp * chunks, chunks), chunks)
+            come = pl.ds(pl.multiple_of((1 - fsdp) * chunks, chunks), chunks)
+            routes = [(base, come, other)]
+        else:
+            size = spans[axis]
+            start = me // size * size
+            routes = []
+            for hop in (1, -1, 2):
+                there = lax.rem(here[axis] + hop + side, side) - here[axis]
+                back = lax.rem(here[axis] - hop + side, side) - here[axis]
+                routes.append((
+                    pl.ds(start, size), pl.ds(start + back * size, size), (fsdp, ctx + there * size)
+                ))
+        copies = []
+        for n, (base, come, where) in enumerate(routes):
+            made = pltpu.make_async_remote_copy(
+                src_ref=tok.at[base], dst_ref=tok.at[base],
+                send_sem=tok_sems.at[0, phase, n], recv_sem=tok_sems.at[1, phase, n],
+                device_id=where, device_id_type=MESH,
+            )
+            made.start()
+            copies.append((made, come))
+
+        def arrive():
+            for n, (made, come) in enumerate(copies):
+                pltpu.make_async_copy(tok.at[come], tok.at[come], tok_sems.at[1, phase, n]).wait()
+                made.wait_send()
+
+        return arrive
+
+    tok[me] = tok_mine[...]
     load_cot.wait()
-    tokens = tok_mine[...].astype(F32)
-
-    def encode(step, _):
-        heads = []
+
+    def pack(step, _):
         for i in range(16):
             r = step * 16 + i
-            code, level = fixed(cot[slab_rows(r), :])
-            cot_out[slab_rows(r), :] = code
-            heads += [tokens, level]
-        head_out[pl.ds(pl.multiple_of(step * 32, 32), 32), :] = jnp.concatenate(heads, axis=0)
+            encode(cot_out, r, cot[slab_rows(r), :])
         return 0
 
-    lax.fori_loop(0, rows // 16, encode, 0)
+    lax.fori_loop(0, rows // 16, pack, 0)
     pl.semaphore_wait(barrier, rows - 1)
-    each_peer(lambda place, where: send(head_out.at[pair(place)], head_in.at[pair(me)], head_sems, where))
-    each_peer(lambda place, where: send(cot_out.at[slab_rows(place)], cot_in.at[slab_rows(me)], cot_sems, where))
-    head_in[pair(me), :] = head_out[pair(me), :]
-    cot_in[slab_rows(me), :] = cot_out[slab_rows(me), :]
+    arrive = exchange(0)
 
     def wait_bytes(ref, sem):
         pltpu.make_async_copy(ref, ref, sem).wait()
@@ -274,6 +304,9 @@
     columns = turned[sub, :LANES]
     for j in range(10):
         taps[j] = jnp.broadcast_to(columns[:, 3 * modes + j : 3 * modes + j + 1], (slab, LANES))
+
+    arrive()
+    arrive = exchange(1)
 
     spread = (iota((slab * modes, slab), 0) // modes == iota((slab * modes, slab), 1)).astype(F32)
     pick = iota((slab * modes, modes), 0) % modes == iota((slab * modes, modes), 1)
@@ -299,6 +332,9 @@
     kernel_head = jnp.sum((up[0] * weight).reshape(slab, modes, LANES), axis=1)
     kernel_head = kernel_head + jnp.where(iota((slab, LANES), 1) == 0, taps[9], 0.0)
 
+    arrive()
+    arrive = exchange(2)
+
     upper = iota((LANES, LANES), 1) >= iota((LANES, LANES), 0)
     for c in range(slab):
         line = jnp.broadcast_to(kernel_head[c : c + 1], (LANES, LANES))
@@ -307,6 +343,9 @@
         toeplitz[0, c] = high
         toeplitz[1, c] = low
 
+    arrive()
+    arrive = exchange(3)
+
     eye = iota((wide, LANES), 0) == iota((wide, LANES), 1)
     step_row = iota((8, LANES), 0)
     steps = jnp.where(step_row == 6, 1, LANES * (1 << jnp.minimum(step_row, 5)))
@@ -325,13 +364,13 @@
 
     diag[...] = jnp.zeros_like(diag)
 
-    wait_bytes(head_in.at[pl.ds(0, 2 * (rows - 1))], head_sems.at[1])
+    arrive()
     lane_c = iota((slab, LANES), 1)
     low_row = iota((LANES, LANES), 0)
     banks = vocab // LANES
 
     def token_parts(r):
-        token = (head_in[pl.ds(2 * r, 1), :] + 0.5).astype(jnp.int32)
+        token = tok[r]
         bank_of = token // LANES
         hot = jnp.where(low_row == token - bank_of * LANES, 1.0, 0.0).astype(BF16)
         return hot, bank_of
@@ -364,8 +403,25 @@
             mix[at, :] = k * v
         return last_one, last_two
 
+    def send_cot(place, where):
+        send(cot_out.at[place, sent_rows], cot_in.at[me, sent_rows], cot_sems, where)
+
+    def lookup(step, carry):
+        per = chunks * UNROLL // rows
+        for n in range(1, per + 1):
+            i = step * per + n
+            there = ctx + i
+            there = jnp.where(there >= chunks, there - chunks, there)
+            send_cot((1 - fsdp) * chunks + there, (1 - fsdp, there))
+            if n < per:
+                send_cot(fsdp * chunks + there, (fsdp, there))
+            else:
+                pl.when(i < chunks)(lambda: send_cot(fsdp * chunks + there, (fsdp, there)))
+        return gather(step, carry)
+
     zero = jnp.zeros((slab, LANES), F32)
-    lax.fori_loop(0, rows // UNROLL, gather, (zero, zero))
+    cot_in[me] = cot_out[me]
+    lax.fori_loop(0, rows // UNROLL, lookup, (zero, zero))
 
     row_in_seq = iota((rows, LANES), 0) % chunks
 
@@ -424,28 +480,24 @@
 
     long_conv(mix, long_out, False)
 
-    def emit(place, where):
+    def emit(place):
         at = slab_rows(place)
-        mixed_out[at, :], level_out[place] = fixed(query[at, :] * long_out[at, :])
-        send(mixed_out.at[at], mixer.at[slab_rows(me)], mixer_sems, where)
-        send(level_out.at[place], mixer_scale.at[me], level_sems, where)
-
-    each_peer(emit)
-    at = slab_rows(me)
-    mixer[at, :], mixer_scale[me] = fixed(query[at, :] * long_out[at, :])
-    most = pl.ds(0, (rows - 1) * slab)
-    wait_bytes(cot_in.at[most], cot_sems.at[1])
-
-    def weigh(step, _):
-        for i in range(8):
-            r = step * 8 + i
-            at = slab_rows(r)
-            value_in = real(cot_in[at, :], head_in[pl.ds(2 * r + 1, 1), :])
-            cot[at, :] = value_in
-            mix[at, :] = value_in * query[at, :]
-        return 0
-
-    lax.fori_loop(0, rows // 8, weigh, 0)
+        q = query[at, :]
+        encode(mixed_out, place, q * long_out[at, :])
+        power_of = cot_in[place, slab:, :].astype(jnp.int32)[:1].astype(F32)
+        value_in = cot_in[place, :slab, :].astype(jnp.int32).astype(F32) * jnp.exp2(power_of)
+        cot[at, :] = value_in
+        mix[at, :] = value_in * q
+
+    def emit_send(place, where):
+        emit(place)
+        send(mixed_out.at[place, sent_rows], mixer.at[me, sent_rows], mixer_sems, where)
+
+    most = pl.ds(0, rows - 1)
+    wait_bytes(cot_in.at[most, sent_rows], cot_sems.at[1])
+    each_peer(emit_send)
+    emit(me)
+    mixer[me] = mixed_out[me]
 
     grad_mixed = query
     long_conv(mix, grad_mixed, True)
@@ -487,11 +539,9 @@
     gather_grad(
         pieces, chunks, quarters, columns_of, every, scales, turn_sems, send_sems, recv_sems
     )
-    wait_bytes(head_in.at[pl.ds(0, 2 * (rows - 1))], head_sems.at[0])
-    wait_bytes(cot_in.at[most], cot_sems.at[0])
+    wait_bytes(cot_in.at[most, sent_rows], cot_sems.at[0])
     for end in range(2):
-        wait_bytes(mixer.at[most], mixer_sems.at[end])
-        wait_bytes(mixer_scale.at[pl.ds(0, rows - 1)], level_sems.at[end])
+        wait_bytes(mixer.at[most, sent_rows], mixer_sems.at[end])
 
 
 def run_block(tok, embedding, conv_taps, gains, residues, decays, seeds, cot, chunks):
@@ -507,19 +557,16 @@
     return pl.pallas_call(
         functools.partial(block_kernel, chunks, chunks * LANES),
         out_shape=(
-            jax.ShapeDtypeStruct((tall, LANES), jnp.int16),
-            jax.ShapeDtypeStruct((rows, 1, LANES), F32),
+            jax.ShapeDtypeStruct((rows, slab + 16, LANES), jnp.int16),
             jax.ShapeDtypeStruct((side,) * 3 + (8, LANES // 8, LANES), jnp.int16),
             jax.ShapeDtypeStruct((side,) * 3 + (1, LANES), F32),
         ),
         in_specs=[vmem, hbm, hbm, vmem, hbm, hbm, hbm, hbm],
-        out_specs=(vmem, vmem, vmem, vmem),
+        out_specs=(vmem, vmem, vmem),
         scratch_shapes=[pltpu.VMEM((tall, LANES), F32)] * 6
-        + [pltpu.VMEM((tall, LANES), jnp.int16)] * 3
+        + [pltpu.VMEM((rows, slab + 16, LANES), jnp.int16)] * 3
         + [
-            pltpu.VMEM((rows, 1, LANES), F32),
-            pltpu.VMEM((2 * rows, LANES), F32),
-            pltpu.VMEM((2 * rows, LANES), F32),
+            pltpu.VMEM((rows, 1, LANES), jnp.int32),
             pltpu.VMEM((2, slab, LANES, LANES), BF16),
             pltpu.VMEM((vocab // LANES * slab, LANES), BF16),
             pltpu.VMEM((10, slab, LANES), F32),
@@ -535,7 +582,7 @@
             pltpu.VMEM((slab // GROUP, 2, 8, LANES), F32),
             pltpu.VMEM((side, slab, LANES), F32),
             pltpu.VMEM((LANES, LANES), F32),
-            dma((6,)), dma((2,)), dma((2,)), dma((2,)), dma((2,)), dma((2, 3)), dma((3, 3, 7)), dma((3, 3, 7)),
+            dma((6,)), dma((2, 4, 3)), dma((2,)), dma((2,)), dma((2, 3)), dma((3, 3, 7)), dma((3, 3, 7)),
         ],
         compiler_params=pltpu.CompilerParams(
             vmem_limit_bytes=56 * 1024 * 1024, collective_id=0, has_side_effects=True
@@ -544,41 +591,41 @@
     )(tok, embedding, conv_taps, gains, residues, decays, seeds, cot)
 
 
-def finish_kernel(every, scales, mixer, mixer_scale, grad_out, mixer_out):
+def finish_kernel(every, scales, mixer, grad_out, mixer_out):
     for z in range(every.shape[0]):
         for x in range(every.shape[1]):
             n = z * every.shape[1] + x
             values = every[z, x, 0].reshape(LANES, LANES).astype(jnp.int32).astype(F32)
             grad_out[:, n * LANES : (n + 1) * LANES] = values * scales[z, x, 0]
-    count = mixer_scale.shape[0]
-    slab = mixer.shape[0] // count
-    for n in range(count):
-        at = slice(n * slab, (n + 1) * slab)
-        mixer_out[at, :] = mixer[at, :].astype(jnp.int32).astype(F32) * mixer_scale[n]
-
-
-def finish(mixer, mixer_scale, every, scales):
+    slab = mixer.shape[1] - 16
+    for n in range(mixer.shape[0]):
+        power_of = mixer[n, slab:, :].astype(jnp.int32)[:1].astype(F32)
+        value = mixer[n, :slab, :].astype(jnp.int32).astype(F32)
+        mixer_out[n * slab : (n + 1) * slab, :] = value * jnp.exp2(power_of)
+
+
+def finish(mixer, every, scales):
     a, b, c, tiles = every.shape[:4]
-    tall, blocks = mixer.shape[0], mixer_scale.shape[0]
+    blocks, slab = mixer.shape[0], mixer.shape[1] - 16
+    tall = blocks * slab
     return pl.pallas_call(
         finish_kernel,
         grid=(c,),
         out_shape=(
             jax.ShapeDtypeStruct((c * LANES, a * b * LANES), F32),
-            jax.ShapeDtypeStruct(mixer.shape, F32),
+            jax.ShapeDtypeStruct((tall, LANES), F32),
         ),
         in_specs=[
             pl.BlockSpec((a, b, 1, *every.shape[3:]), lambda n: (0, 0, n, 0, 0, 0)),
             pl.BlockSpec((a, b, 1, 1, LANES), lambda n: (0, 0, n, 0, 0)),
-            pl.BlockSpec((tall // c, LANES), lambda n: (n, 0)),
-            pl.BlockSpec((blocks // c, 1, LANES), lambda n: (n, 0, 0)),
+            pl.BlockSpec((blocks // c, *mixer.shape[1:]), lambda n: (n, 0, 0)),
         ],
         out_specs=(
             pl.BlockSpec((LANES, a * b * LANES), lambda n: (n, 0)),
             pl.BlockSpec((tall // c, LANES), lambda n: (n, 0)),
         ),
         name="finish",
-    )(every, scales, mixer, mixer_scale)
+    )(every, scales, mixer)
 
 
 def body(token_ids, embedding, conv_taps, residues, decays, filter_seed, skip_gain, cotangent):

time: 78.7 us -> 92.3 us (1.17)
  Pallas kernels: 77.5 us -> 91.4 us
    pallas_call x1, Pallas kernels: 72.3 us -> 86.1 us  [run_block(): pl.pallas_call(functools.partial(block_kernel, chunks, chunks * LANES), o...]
where the time goes in v6:
time: 92.3 us; the launch traced here: 92 us
  Pallas kernels  91.4 us (99%)
    pallas_call x1, Pallas kernels, run_block(): pl.pallas_call(functools.partial(block_kernel, chunks, chunks * LANES), o...  86.1 us
    pallas_call x1, Pallas kernels, finish(): pl.pallas_call(finish_kernel, grid=(c,), out_shape=(jax.ShapeDtypeStruct(...  5.26 us

profile of v6, /device:TPU:0, one launch (start us, length us, event | category | flops | bytes accessed | tf_op | source)
XLA Modules:
  0.0 92.0 jit_solution(4882488574453663372)
XLA Ops:
  0.6 86.1 %hyena_block.1 = (s16[128,48,128]{2,1,0:T(8,128)(2,1)}, s16[4,4,4,8,16,128]{5,4,3,2,1,0:T(8,128)(2,1)}, f32[4,4,4,1,128]{4,3,2,1,0:T(1,128)}) custom-call(s32[1,128]{1,0:T(1,128)} %tok_mine.1, bf16[512,2048]{1,0:T(8,128)(2,1)} %embedding.1, f32[3,3,4096]{2,1,0:T(4,128)} %conv_taps.1, f32[32,128]{1,0:T(8,128)} %bitcast.10, f32[16,4096]{1,0:T(8,128)} %bitcast.7, ...), custom_call_target="tpu_custom_call" | custom-call | tf_op jit(solution)/shard_map/hyena_block/pallas_call | solution.py:557
  86.8 5.3 %finish.1 = (f32[512,2048]{1,0:T(8,128)}, f32[4096,128]{1,0:T(8,128)}) custom-call(s16[4,4,4,8,16,128]{5,4,3,2,1,0:T(8,128)(2,1)} %get-tuple-element.7.every, f32[4,4,4,1,128]{4,3,2,1,0:T(1,128)} %get-tuple-element.8.scales, s16[128,48,128]{2,1,0:T(8,128)(2,1)} %get-tuple-element.9.mixer), custom_call_target="tpu_custom_call" | custom-call | tf_op jit(solution)/shard_map/finish/pallas_call | solution.py:611

commit v7 on v6

--- a/solution.py
+++ b/solution.py
@@ -67,7 +67,19 @@
 LEVELS = 32767.0
 
 
-def gather_grad(pieces, chunks, quarters, columns_of, every, scales, turn_sems, send_sems, recv_sems):
+def fixed(block):
+    peak = jnp.maximum(jnp.max(jnp.abs(block), axis=0, keepdims=True), 1e-30)
+    power_of = jnp.ceil(jnp.log2(peak * (1.0 / LEVELS)))
+    code = jnp.clip(jnp.round(block * jnp.exp2(-power_of)), -LEVELS, LEVELS)
+    return code.astype(jnp.int32).astype(jnp.int16), power_of
+
+
+def real(code, power_of):
+    scale = jnp.exp2(power_of.astype(jnp.int32)[:1].astype(F32))
+    return code.astype(jnp.int32).astype(F32) * scale
+
+
+def gather_grad(pieces, chunks, quarters, columns_of, every, turn_sems, send_sems, recv_sems):
     sides = every.shape[:3]
     ctx = lax.axis_index("ctx")
     fsdp = lax.axis_index("fsdp")
@@ -102,13 +114,12 @@
         there = neighbour(2, hop)[0]
         landed(columns_of.at[pl.ds(pl.multiple_of(there * slab, slab), slab)], turn_sems.at[1, n])
     block = columns_of[...].T
-    peak = jnp.max(jnp.abs(block), axis=0, keepdims=True)
-    block = jnp.round(block * (LEVELS / jnp.maximum(peak, 1e-30))).astype(jnp.int32).astype(jnp.int16)
-    tiles = every.shape[3]
-    every[here[0], here[1], here[2]] = block.reshape(tiles, LANES // tiles, LANES)
-    scales[here[0], here[1], here[2]] = peak * (1.0 / LEVELS)
-
-    def at(ref, axis, hop, done, *rest):
+    code, power_of = fixed(block)
+    tiles, height = every.shape[3] - 1, every.shape[4]
+    every[here[0], here[1], here[2], :tiles] = code.reshape(tiles, height, LANES)
+    every[here[0], here[1], here[2], tiles] = jnp.broadcast_to(power_of, (height, LANES)).astype(jnp.int32).astype(jnp.int16)
+
+    def at(axis, hop, done, part):
         index = []
         for n in range(3):
             if n == axis:
@@ -117,50 +128,18 @@
                 index.append(slice(None))
             else:
                 index.append(pl.ds(here[n], 1))
-        return ref.at[(*index, *rest)]
-
-    third = -(-tiles // 3)
-    cuts = (0, third, 2 * third, tiles)
+        third = (tiles + 1) // 3
+        return every.at[(*index, pl.ds(part * third, third))]
+
     for phase in range(3):
-        plan = []
-        for part in range(3):
-            order = [(2 - part + n) % 3 for n in range(3)]
-            axis, done = order[phase], order[:phase]
-            first, size = cuts[part], cuts[part + 1] - cuts[part]
-            half = size // 2
-            whole, low, high = pl.ds(first, size), pl.ds(first, half), pl.ds(first + half, size - half)
-            plan.append((part, axis, done, whole, low, high))
-            right, left = neighbour(axis, 1)[1], neighbour(axis, -1)[1]
-            mine = at(every, axis, 0, done, whole)
-            sems = (send_sems.at[part, phase], recv_sems.at[part, phase])
-            send(mine, mine, sems[0].at[0], sems[1].at[0], right)
-            send(mine, mine, sems[0].at[1], sems[1].at[1], left)
-            if phase < 2:
-                send(mine, mine, sems[0].at[2], sems[1].at[2], neighbour(axis, 2)[1])
-            if part == 2:
-                level = at(scales, axis, 0, done)
-                for n, hop in enumerate((1, -1, 2)):
-                    send(level, level, sems[0].at[4 + n], sems[1].at[4 + n], neighbour(axis, hop)[1])
-        for part, axis, done, whole, low, high in plan:
-            sems = (send_sems.at[part, phase], recv_sems.at[part, phase])
-            landed(at(every, axis, -1, done, whole), sems[1].at[0])
-            if phase == 2:
-                piece = at(every, axis, -1, done, low)
-                send(piece, piece, sems[0].at[2], sems[1].at[2], neighbour(axis, 1)[1])
-            landed(at(every, axis, 1, done, whole), sems[1].at[1])
-            if phase == 2:
-                piece = at(every, axis, 1, done, high)
-                send(piece, piece, sems[0].at[3], sems[1].at[3], neighbour(axis, -1)[1])
-        for part, axis, done, whole, low, high in plan:
-            sem = recv_sems.at[part, phase]
-            if phase < 2:
-                landed(at(every, axis, 2, done, whole), sem.at[2])
-            else:
-                landed(at(every, axis, 2, done, low), sem.at[2])
-                landed(at(every, axis, 2, done, high), sem.at[3])
-            if part == 2:
-                for n, hop in enumerate((-1, 1, 2)):
-                    landed(at(scales, axis, hop, done), sem.at[4 + n])
+        plan = [((2 - part + phase) % 3, [(2 - part + n) % 3 for n in range(phase)]) for part in range(3)]
+        for part, (axis, done) in enumerate(plan):
+            mine = at(axis, 0, done, part)
+            for n, hop in enumerate((2, 1, -1)):
+                send(mine, mine, send_sems.at[part, phase, n], recv_sems.at[part, phase, n], neighbour(axis, hop)[1])
+        for part, (axis, done) in enumerate(plan):
+            for n, hop in enumerate((2, -1, 1)):
+                landed(at(axis, hop, done, part), recv_sems.at[part, phase, n])
     for made in sent:
         made.wait_send()
 
@@ -168,7 +147,7 @@
 def block_kernel(
     chunks, seq_len,
     tok_mine, embedding, conv_taps, gains, residue_all, decay_all, seed_all, cot_mine,
-    mixer, every, scales,
+    mixer, every,
     query, key, value, mix, long_out, cot, cot_out, cot_in, mixed_out, tok,
     staged, table, taps, residues, decays, seeds, raw_table, turned, raw_taps,
     bank, toeplitz, diag, state_rows, quarters, columns_of,
@@ -229,52 +208,11 @@
     sent_rows = pl.ds(0, slab + 2)
 
     def encode(target, place, block):
-        peak = jnp.maximum(jnp.max(jnp.abs(block), axis=0, keepdims=True), 1e-30)
-        power_of = jnp.ceil(jnp.log2(peak * (1.0 / LEVELS)))
-        code = jnp.clip(jnp.round(block * jnp.exp2(-power_of)), -LEVELS, LEVELS)
-        target[place, :slab, :] = code.astype(jnp.int32).astype(jnp.int16)
-        exponent = jnp.broadcast_to(power_of, (16, LANES)).astype(jnp.int32).astype(jnp.int16)
-        target[place, slab:, :] = exponent
-
-    side = round(chunks ** (1 / 3))
-    here = (ctx // (side * side), lax.rem(ctx // side, side), lax.rem(ctx, side))
-    spans = (side * side, side, 1)
-
-    def exchange(phase):
-        axis = 2 - phase
-        if axis < 0:
-            other = (1 - fsdp, ctx)
-            base = pl.ds(pl.multiple_of(fsdp * chunks, chunks), chunks)
-            come = pl.ds(pl.multiple_of((1 - fsdp) * chunks, chunks), chunks)
-            routes = [(base, come, other)]
-        else:
-            size = spans[axis]
-            start = me // size * size
-            routes = []
-            for hop in (1, -1, 2):
-                there = lax.rem(here[axis] + hop + side, side) - here[axis]
-                back = lax.rem(here[axis] - hop + side, side) - here[axis]
-                routes.append((
-                    pl.ds(start, size), pl.ds(start + back * size, size), (fsdp, ctx + there * size)
-                ))
-        copies = []
-        for n, (base, come, where) in enumerate(routes):
-            made = pltpu.make_async_remote_copy(
-                src_ref=tok.at[base], dst_ref=tok.at[base],
-                send_sem=tok_sems.at[0, phase, n], recv_sem=tok_sems.at[1, phase, n],
-                device_id=where, device_id_type=MESH,
-            )
-            made.start()
-            copies.append((made, come))
-
-        def arrive():
-            for n, (made, come) in enumerate(copies):
-                pltpu.make_async_copy(tok.at[come], tok.at[come], tok_sems.at[1, phase, n]).wait()
-                made.wait_send()
-
-        return arrive
-
-    tok[me] = tok_mine[...]
+        code, power_of = fixed(block)
+        target[place, :slab, :] = code
+        target[place, slab:, :] = jnp.broadcast_to(power_of, (16, LANES)).astype(jnp.int32).astype(jnp.int16)
+
+    own_tok = tok_mine[...]
     load_cot.wait()
 
     def pack(step, _):
@@ -285,7 +223,19 @@
 
     lax.fori_loop(0, rows // 16, pack, 0)
     pl.semaphore_wait(barrier, rows - 1)
-    arrive = exchange(0)
+    tok[me] = own_tok
+
+    def send_tok(i, _):
+        there = ctx + i
+        there = jnp.where(there >= chunks, there - chunks, there)
+        send(tok_mine, tok.at[me], tok_sems.at[0], (fsdp, there))
+        return 0
+
+    lax.fori_loop(1, chunks, send_tok, 0, unroll=7)
+    def send_cot(place, where):
+        send(cot_out.at[place, sent_rows], cot_in.at[me, sent_rows], cot_sems, where)
+
+    each_peer(send_cot)
 
     def wait_bytes(ref, sem):
         pltpu.make_async_copy(ref, ref, sem).wait()
@@ -304,9 +254,6 @@
     columns = turned[sub, :LANES]
     for j in range(10):
         taps[j] = jnp.broadcast_to(columns[:, 3 * modes + j : 3 * modes + j + 1], (slab, LANES))
-
-    arrive()
-    arrive = exchange(1)
 
     spread = (iota((slab * modes, slab), 0) // modes == iota((slab * modes, slab), 1)).astype(F32)
     pick = iota((slab * modes, modes), 0) % modes == iota((slab * modes, modes), 1)
@@ -332,9 +279,6 @@
     kernel_head = jnp.sum((up[0] * weight).reshape(slab, modes, LANES), axis=1)
     kernel_head = kernel_head + jnp.where(iota((slab, LANES), 1) == 0, taps[9], 0.0)
 
-    arrive()
-    arrive = exchange(2)
-
     upper = iota((LANES, LANES), 1) >= iota((LANES, LANES), 0)
     for c in range(slab):
         line = jnp.broadcast_to(kernel_head[c : c + 1], (LANES, LANES))
@@ -343,9 +287,6 @@
         toeplitz[0, c] = high
         toeplitz[1, c] = low
 
-    arrive()
-    arrive = exchange(3)
-
     eye = iota((wide, LANES), 0) == iota((wide, LANES), 1)
     step_row = iota((8, LANES), 0)
     steps = jnp.where(step_row == 6, 1, LANES * (1 << jnp.minimum(step_row, 5)))
@@ -364,7 +305,9 @@
 
     diag[...] = jnp.zeros_like(diag)
 
-    arrive()
+    wait_bytes(tok.at[pl.ds(0, chunks - 1)], tok_sems.at[0, 1])
+    own_half = tok.at[pl.ds(pl.multiple_of(fsdp * chunks, chunks), chunks)]
+    send(own_half, own_half, tok_sems.at[1], (1 - fsdp, ctx))
     lane_c = iota((slab, LANES), 1)
     low_row = iota((LANES, LANES), 0)
     banks = vocab // LANES
@@ -377,14 +320,11 @@
 
     UNROLL = 16
 
-    def gather(step, carry):
+    def gather(base, step, carry):
         last_one, last_two = carry
-        r0 = step * UNROLL
+        r0 = base + step * UNROLL
         parts = [token_parts(r0 + i) for i in range(UNROLL)]
         found = nn(table[...], jnp.concatenate([hot for hot, _ in parts], axis=1))
-        fresh = (r0 % chunks) == 0
-        last_one = jnp.where(fresh, 0.0, last_one)
-        last_two = jnp.where(fresh, 0.0, last_two)
         for i in range(UNROLL):
             bank_of = parts[i][1]
             x = found[:slab, i * LANES : (i + 1) * LANES]
@@ -403,25 +343,12 @@
             mix[at, :] = k * v
         return last_one, last_two
 
-    def send_cot(place, where):
-        send(cot_out.at[place, sent_rows], cot_in.at[me, sent_rows], cot_sems, where)
-
-    def lookup(step, carry):
-        per = chunks * UNROLL // rows
-        for n in range(1, per + 1):
-            i = step * per + n
-            there = ctx + i
-            there = jnp.where(there >= chunks, there - chunks, there)
-            send_cot((1 - fsdp) * chunks + there, (1 - fsdp, there))
-            if n < per:
-                send_cot(fsdp * chunks + there, (fsdp, there))
-            else:
-                pl.when(i < chunks)(lambda: send_cot(fsdp * chunks + there, (fsdp, there)))
-        return gather(step, carry)
-
     zero = jnp.zeros((slab, LANES), F32)
     cot_in[me] = cot_out[me]
-    lax.fori_loop(0, rows // UNROLL, lookup, (zero, zero))
+    per_sequence = chunks // UNROLL
+    lax.fori_loop(0, per_sequence, functools.partial(gather, fsdp * chunks), (zero, zero))
+    wait_bytes(own_half, tok_sems.at[1, 1])
+    lax.fori_loop(0, per_sequence, functools.partial(gather, (1 - fsdp) * chunks), (zero, zero))
 
     row_in_seq = iota((rows, LANES), 0) % chunks
 
@@ -484,19 +411,22 @@
         at = slab_rows(place)
         q = query[at, :]
         encode(mixed_out, place, q * long_out[at, :])
-        power_of = cot_in[place, slab:, :].astype(jnp.int32)[:1].astype(F32)
-        value_in = cot_in[place, :slab, :].astype(jnp.int32).astype(F32) * jnp.exp2(power_of)
+        value_in = real(cot_in[place, :slab, :], cot_in[place, slab:, :])
         cot[at, :] = value_in
         mix[at, :] = value_in * q
 
     def emit_send(place, where):
-        emit(place)
         send(mixed_out.at[place, sent_rows], mixer.at[me, sent_rows], mixer_sems, where)
 
     most = pl.ds(0, rows - 1)
     wait_bytes(cot_in.at[most, sent_rows], cot_sems.at[1])
+    def emit_step(step, _):
+        for i in range(8):
+            emit(step * 8 + i)
+        return 0
+
+    lax.fori_loop(0, rows // 8, emit_step, 0)
     each_peer(emit_send)
-    emit(me)
     mixer[me] = mixed_out[me]
 
     grad_mixed = query
@@ -537,9 +467,11 @@
     step = 2 * slab
     pieces = [total[b * step : b * step + slab] + total[b * step + slab : (b + 1) * step] for b in range(banks)]
     gather_grad(
-        pieces, chunks, quarters, columns_of, every, scales, turn_sems, send_sems, recv_sems
+        pieces, chunks, quarters, columns_of, every, turn_sems, send_sems, recv_sems
     )
     wait_bytes(cot_in.at[most, sent_rows], cot_sems.at[0])
+    wait_bytes(tok.at[pl.ds(0, chunks - 1)], tok_sems.at[0, 0])
+    wait_bytes(own_half, tok_sems.at[1, 0])
     for end in range(2):
         wait_bytes(mixer.at[most, sent_rows], mixer_sems.at[end])
 
@@ -558,11 +490,10 @@
         functools.partial(block_kernel, chunks, chunks * LANES),
         out_shape=(
             jax.ShapeDtypeStruct((rows, slab + 16, LANES), jnp.int16),
-            jax.ShapeDtypeStruct((side,) * 3 + (8, LANES // 8, LANES), jnp.int16),
-            jax.ShapeDtypeStruct((side,) * 3 + (1, LANES), F32),
+            jax.ShapeDtypeStruct((side,) * 3 + (LANES // 16 + 1, 16, LANES), jnp.int16),
         ),
         in_specs=[vmem, hbm, hbm, vmem, hbm, hbm, hbm, hbm],
-        out_specs=(vmem, vmem, vmem),
+        out_specs=(vmem, vmem),
         scratch_shapes=[pltpu.VMEM((tall, LANES), F32)] * 6
         + [pltpu.VMEM((rows, slab + 16, LANES), jnp.int16)] * 3
         + [
@@ -582,7 +513,7 @@
             pltpu.VMEM((slab // GROUP, 2, 8, LANES), F32),
             pltpu.VMEM((side, slab, LANES), F32),
             pltpu.VMEM((LANES, LANES), F32),
-            dma((6,)), dma((2, 4, 3)), dma((2,)), dma((2,)), dma((2, 3)), dma((3, 3, 7)), dma((3, 3, 7)),
+            dma((6,)), dma((2, 2)), dma((2,)), dma((2,)), dma((2, 3)), dma((3, 3, 3)), dma((3, 3, 3)),
         ],
         compiler_params=pltpu.CompilerParams(
             vmem_limit_bytes=56 * 1024 * 1024, collective_id=0, has_side_effects=True
@@ -591,41 +522,42 @@
     )(tok, embedding, conv_taps, gains, residues, decays, seeds, cot)
 
 
-def finish_kernel(every, scales, mixer, grad_out, mixer_out):
+def finish_kernel(every, powers, mixer, grad_out, mixer_out):
+    height = grad_out.shape[0]
     for z in range(every.shape[0]):
         for x in range(every.shape[1]):
             n = z * every.shape[1] + x
-            values = every[z, x, 0].reshape(LANES, LANES).astype(jnp.int32).astype(F32)
-            grad_out[:, n * LANES : (n + 1) * LANES] = values * scales[z, x, 0]
+            grad_out[:, n * LANES : (n + 1) * LANES] = real(every[z, x, 0].reshape(height, LANES), powers[z, x, 0, 0])
     slab = mixer.shape[1] - 16
     for n in range(mixer.shape[0]):
-        power_of = mixer[n, slab:, :].astype(jnp.int32)[:1].astype(F32)
-        value = mixer[n, :slab, :].astype(jnp.int32).astype(F32)
-        mixer_out[n * slab : (n + 1) * slab, :] = value * jnp.exp2(power_of)
-
-
-def finish(mixer, every, scales):
-    a, b, c, tiles = every.shape[:4]
+        mixer_out[n * slab : (n + 1) * slab, :] = real(mixer[n, :slab, :], mixer[n, slab:, :])
+
+
+def finish(mixer, every):
+    a, b, c, tiles, height = every.shape[:5]
     blocks, slab = mixer.shape[0], mixer.shape[1] - 16
     tall = blocks * slab
+    cuts = 1
+    part = (tiles - 1) // cuts
+    steps = c * cuts
     return pl.pallas_call(
         finish_kernel,
-        grid=(c,),
+        grid=(steps,),
         out_shape=(
             jax.ShapeDtypeStruct((c * LANES, a * b * LANES), F32),
             jax.ShapeDtypeStruct((tall, LANES), F32),
         ),
         in_specs=[
-            pl.BlockSpec((a, b, 1, *every.shape[3:]), lambda n: (0, 0, n, 0, 0, 0)),
-            pl.BlockSpec((a, b, 1, 1, LANES), lambda n: (0, 0, n, 0, 0)),
-            pl.BlockSpec((blocks // c, *mixer.shape[1:]), lambda n: (n, 0, 0)),
+            pl.BlockSpec((a, b, 1, part, height, LANES), lambda n: (0, 0, n // cuts, n % cuts, 0, 0)),
+            pl.BlockSpec((a, b, 1, 1, height, LANES), lambda n: (0, 0, n // cuts, tiles - 1, 0, 0)),
+            pl.BlockSpec((blocks // steps, *mixer.shape[1:]), lambda n: (n, 0, 0)),
         ],
         out_specs=(
-            pl.BlockSpec((LANES, a * b * LANES), lambda n: (n, 0)),
-            pl.BlockSpec((tall // c, LANES), lambda n: (n, 0)),
+            pl.BlockSpec((LANES // cuts, a * b * LANES), lambda n: (n, 0)),
+            pl.BlockSpec((tall // steps, LANES), lambda n: (n, 0)),
         ),
         name="finish",
-    )(every, scales, mixer)
+    )(every, every, mixer)
 
 
 def body(token_ids, embedding, conv_taps, residues, decays, filter_seed, skip_gain, cotangent):

time: 92.3 us -> 75.6 us (0.82)
  Pallas kernels: 91.4 us -> 74.7 us
    pallas_call x1, Pallas kernels: 86.1 us -> 69.3 us  [run_block(): pl.pallas_call(functools.partial(block_kernel, chunks, chunks * LANES), o...]
where the time goes in v7:
time: 75.6 us; the launch traced here: 75.3 us
  Pallas kernels  74.7 us (99%)
    pallas_call x1, Pallas kernels, run_block(): pl.pallas_call(functools.partial(block_kernel, chunks, chunks * LANES), o...  69.3 us
    pallas_call x1, Pallas kernels, finish(): pl.pallas_call(finish_kernel, grid=(steps,), out_shape=(jax.ShapeDtypeStr...  5.33 us

profile of v7, /device:TPU:0, one launch (start us, length us, event | category | flops | bytes accessed | tf_op | source)
XLA Modules:
  0.0 75.3 jit_solution(2548555100325996835)
XLA Ops:
  0.6 69.3 %hyena_block.1 = (s16[128,48,128]{2,1,0:T(8,128)(2,1)}, s16[4,4,4,9,16,128]{5,4,3,2,1,0:T(8,128)(2,1)}) custom-call(s32[1,128]{1,0:T(1,128)} %tok_mine.1, bf16[512,2048]{1,0:T(8,128)(2,1)} %embedding.1, f32[3,3,4096]{2,1,0:T(4,128)} %conv_taps.1, f32[32,128]{1,0:T(8,128)} %bitcast.10, f32[16,4096]{1,0:T(8,128)} %bitcast.7, f32[16,4096]{1,0:T(8,128)} %bitcast.8, ...), custom_call_target="tpu_custom_call" | custom-call | tf_op jit(solution)/shard_map/hyena_block/pallas_call | solution.py:489
  70.0 5.3 %finish.1 = (f32[512,2048]{1,0:T(8,128)}, f32[4096,128]{1,0:T(8,128)}) custom-call(s16[4,4,4,9,16,128]{5,4,3,2,1,0:T(8,128)(2,1)} %get-tuple-element.6.every.powers, s16[4,4,4,9,16,128]{5,4,3,2,1,0:T(8,128)(2,1)} %get-tuple-element.6.every.powers, s16[128,48,128]{2,1,0:T(8,128)(2,1)} %get-tuple-element.7.mixer), custom_call_target="tpu_custom_call" | custom-call | tf_op jit(solution)/shard_map/finish/pallas_call | solution.py:543

commit v8 on v7

--- a/solution.py
+++ b/solution.py
@@ -148,10 +148,10 @@
     chunks, seq_len,
     tok_mine, embedding, conv_taps, gains, residue_all, decay_all, seed_all, cot_mine,
     mixer, every,
-    query, key, value, mix, long_out, cot, cot_out, cot_in, mixed_out, tok,
+    query, key, value, mix, long_out, cot, cot_away, cot_out, cot_in, mixed_out, mixed_in, tok,
     staged, table, taps, residues, decays, seeds, raw_table, turned, raw_taps,
     bank, toeplitz, diag, state_rows, quarters, columns_of,
-    load_sems, tok_sems, cot_sems, mixer_sems, turn_sems, send_sems, recv_sems,
+    load_sems, tok_sems, cot_sems, mixer_sems, relay_sems, own_sem, turn_sems, send_sems, recv_sems,
 ):
     vocab = embedding.shape[0]
     rows = tok.shape[0]
@@ -167,14 +167,13 @@
     def slab_rows(index):
         return pl.ds(pl.multiple_of(index * slab, slab), slab)
 
+    sibling = (1 - fsdp, ctx)
+
     def each_peer(action):
-        action((1 - fsdp) * chunks + ctx, (1 - fsdp, ctx))
-
         def step(i, _):
             there = ctx + i
             there = jnp.where(there >= chunks, there - chunks, there)
-            for side in (fsdp, 1 - fsdp):
-                action(side * chunks + there, (side, there))
+            action(there, (fsdp, there))
             return 0
 
         lax.fori_loop(1, chunks, step, 0, unroll=7)
@@ -188,6 +187,7 @@
     barrier = pltpu.get_barrier_semaphore()
     load_cot = pltpu.make_async_copy(cot_mine, cot, load_sems.at[5])
     load_cot.start()
+    pl.semaphore_signal(barrier, inc=1, device_id=sibling, device_id_type=MESH)
     each_peer(lambda place, where: pl.semaphore_signal(barrier, inc=1, device_id=where, device_id_type=MESH))
 
     lane_tile = pl.ds(pl.multiple_of(ctx // per_tile * LANES, LANES), LANES)
@@ -207,39 +207,34 @@
 
     sent_rows = pl.ds(0, slab + 2)
 
-    def encode(target, place, block):
+    def encode(target, block):
         code, power_of = fixed(block)
-        target[place, :slab, :] = code
-        target[place, slab:, :] = jnp.broadcast_to(power_of, (16, LANES)).astype(jnp.int32).astype(jnp.int16)
-
-    own_tok = tok_mine[...]
+        target[:slab, :] = code
+        target[slab:, :] = jnp.broadcast_to(power_of, (16, LANES)).astype(jnp.int32).astype(jnp.int16)
+
+    tok[me] = tok_mine[...]
     load_cot.wait()
 
-    def pack(step, _):
+    def pack(half, target, step, _):
         for i in range(16):
-            r = step * 16 + i
-            encode(cot_out, r, cot[slab_rows(r), :])
+            c = step * 16 + i
+            encode(target.at[c], cot[slab_rows(half * chunks + c), :])
         return 0
 
-    lax.fori_loop(0, rows // 16, pack, 0)
-    pl.semaphore_wait(barrier, rows - 1)
-    tok[me] = own_tok
-
-    def send_tok(i, _):
-        there = ctx + i
-        there = jnp.where(there >= chunks, there - chunks, there)
-        send(tok_mine, tok.at[me], tok_sems.at[0], (fsdp, there))
-        return 0
-
-    lax.fori_loop(1, chunks, send_tok, 0, unroll=7)
-    def send_cot(place, where):
-        send(cot_out.at[place, sent_rows], cot_in.at[me, sent_rows], cot_sems, where)
-
-    each_peer(send_cot)
+    lax.fori_loop(0, chunks // 16, functools.partial(pack, 1 - fsdp, cot_away), 0)
+    pl.semaphore_wait(barrier, chunks)
+    send(cot_away.at[:, sent_rows], cot_out.at[:, fsdp, sent_rows], relay_sems.at[0], sibling)
+    each_peer(lambda place, where: send(tok_mine, tok.at[me], tok_sems.at[0], where))
+    lax.fori_loop(0, chunks // 16, functools.partial(pack, fsdp, cot_out.at[:, fsdp]), 0)
 
     def wait_bytes(ref, sem):
         pltpu.make_async_copy(ref, ref, sem).wait()
 
+    wait_bytes(cot_out.at[:, 1 - fsdp, sent_rows], relay_sems.at[0, 1])
+    each_peer(
+        lambda place, where: send(cot_out.at[place, :, sent_rows], cot_in.at[ctx, :, sent_rows], cot_sems, where)
+    )
+    cot_in[ctx] = cot_out[ctx]
     for load in loads:
         load.wait()
     sub = pl.ds(pl.multiple_of(lax.rem(ctx, per_tile) * slab, slab), slab)
@@ -307,7 +302,7 @@
 
     wait_bytes(tok.at[pl.ds(0, chunks - 1)], tok_sems.at[0, 1])
     own_half = tok.at[pl.ds(pl.multiple_of(fsdp * chunks, chunks), chunks)]
-    send(own_half, own_half, tok_sems.at[1], (1 - fsdp, ctx))
+    send(own_half, own_half, tok_sems.at[1], sibling)
     lane_c = iota((slab, LANES), 1)
     low_row = iota((LANES, LANES), 0)
     banks = vocab // LANES
@@ -344,7 +339,6 @@
         return last_one, last_two
 
     zero = jnp.zeros((slab, LANES), F32)
-    cot_in[me] = cot_out[me]
     per_sequence = chunks // UNROLL
     lax.fori_loop(0, per_sequence, functools.partial(gather, fsdp * chunks), (zero, zero))
     wait_bytes(own_half, tok_sems.at[1, 1])
@@ -407,27 +401,28 @@
 
     long_conv(mix, long_out, False)
 
-    def emit(place):
-        at = slab_rows(place)
+    def emit(seq, c):
+        at = slab_rows(seq * chunks + c)
         q = query[at, :]
-        encode(mixed_out, place, q * long_out[at, :])
-        value_in = real(cot_in[place, :slab, :], cot_in[place, slab:, :])
+        encode(mixed_out.at[c, seq], q * long_out[at, :])
+        value_in = real(cot_in[c, seq, :slab, :], cot_in[c, seq, slab:, :])
         cot[at, :] = value_in
         mix[at, :] = value_in * q
 
-    def emit_send(place, where):
-        send(mixed_out.at[place, sent_rows], mixer.at[me, sent_rows], mixer_sems, where)
-
-    most = pl.ds(0, rows - 1)
-    wait_bytes(cot_in.at[most, sent_rows], cot_sems.at[1])
+    most = pl.ds(0, chunks - 1)
+    wait_bytes(cot_in.at[most, :, sent_rows], cot_sems.at[1])
+
     def emit_step(step, _):
-        for i in range(8):
-            emit(step * 8 + i)
+        for i in range(4):
+            for seq in range(2):
+                emit(seq, step * 4 + i)
         return 0
 
-    lax.fori_loop(0, rows // 8, emit_step, 0)
-    each_peer(emit_send)
-    mixer[me] = mixed_out[me]
+    lax.fori_loop(0, chunks // 4, emit_step, 0)
+    each_peer(
+        lambda place, where: send(mixed_out.at[place, :, sent_rows], mixed_in.at[ctx, :, sent_rows], mixer_sems, where)
+    )
+    mixed_in[ctx] = mixed_out[ctx]
 
     grad_mixed = query
     long_conv(mix, grad_mixed, True)
@@ -466,14 +461,21 @@
     )
     step = 2 * slab
     pieces = [total[b * step : b * step + slab] + total[b * step + slab : (b + 1) * step] for b in range(banks)]
+    wait_bytes(mixed_in.at[most, :, sent_rows], mixer_sems.at[1])
+    send(mixed_in.at[:, 1 - fsdp, sent_rows], mixer.at[fsdp, :, sent_rows], relay_sems.at[1], sibling)
+    keep = pltpu.make_async_copy(mixed_in.at[:, fsdp, sent_rows], mixer.at[fsdp, :, sent_rows], own_sem)
+    keep.start()
     gather_grad(
         pieces, chunks, quarters, columns_of, every, turn_sems, send_sems, recv_sems
     )
-    wait_bytes(cot_in.at[most, sent_rows], cot_sems.at[0])
     wait_bytes(tok.at[pl.ds(0, chunks - 1)], tok_sems.at[0, 0])
     wait_bytes(own_half, tok_sems.at[1, 0])
+    wait_bytes(cot_away.at[:, sent_rows], relay_sems.at[0, 0])
+    wait_bytes(cot_in.at[most, :, sent_rows], cot_sems.at[0])
+    wait_bytes(mixed_in.at[most, :, sent_rows], mixer_sems.at[0])
+    keep.wait()
     for end in range(2):
-        wait_bytes(mixer.at[most, sent_rows], mixer_sems.at[end])
+        wait_bytes(mixer.at[1 - fsdp, :, sent_rows], relay_sems.at[1, end])
 
 
 def run_block(tok, embedding, conv_taps, gains, residues, decays, seeds, cot, chunks):
@@ -489,13 +491,14 @@
     return pl.pallas_call(
         functools.partial(block_kernel, chunks, chunks * LANES),
         out_shape=(
-            jax.ShapeDtypeStruct((rows, slab + 16, LANES), jnp.int16),
+            jax.ShapeDtypeStruct((2, chunks, slab + 16, LANES), jnp.int16),
             jax.ShapeDtypeStruct((side,) * 3 + (LANES // 16 + 1, 16, LANES), jnp.int16),
         ),
         in_specs=[vmem, hbm, hbm, vmem, hbm, hbm, hbm, hbm],
         out_specs=(vmem, vmem),
         scratch_shapes=[pltpu.VMEM((tall, LANES), F32)] * 6
-        + [pltpu.VMEM((rows, slab + 16, LANES), jnp.int16)] * 3
+        + [pltpu.VMEM((chunks, slab + 16, LANES), jnp.int16)]
+        + [pltpu.VMEM((chunks, 2, slab + 16, LANES), jnp.int16)] * 4
         + [
             pltpu.VMEM((rows, 1, LANES), jnp.int32),
             pltpu.VMEM((2, slab, LANES, LANES), BF16),
@@ -513,7 +516,7 @@
             pltpu.VMEM((slab // GROUP, 2, 8, LANES), F32),
             pltpu.VMEM((side, slab, LANES), F32),
             pltpu.VMEM((LANES, LANES), F32),
-            dma((6,)), dma((2, 2)), dma((2,)), dma((2,)), dma((2, 3)), dma((3, 3, 3)), dma((3, 3, 3)),
+            dma((6,)), dma((2, 2)), dma((2,)), dma((2,)), dma((2, 2)), dma, dma((2, 3)), dma((3, 3, 3)), dma((3, 3, 3)),
         ],
         compiler_params=pltpu.CompilerParams(
             vmem_limit_bytes=56 * 1024 * 1024, collective_id=0, has_side_effects=True
@@ -535,6 +538,7 @@
 
 def finish(mixer, every):
     a, b, c, tiles, height = every.shape[:5]
+    mixer = mixer.reshape(-1, *mixer.shape[2:])
     blocks, slab = mixer.shape[0], mixer.shape[1] - 16
     tall = blocks * slab
     cuts = 1

time: 75.6 us -> 81.6 us (1.079)
  Pallas kernels: 74.7 us -> 80.7 us
    pallas_call x1, Pallas kernels: 69.3 us -> 75.3 us  [run_block(): pl.pallas_call(functools.partial(block_kernel, chunks, chunks * LANES), o...]
where the time goes in v8:
time: 81.6 us; the launch traced here: 81.3 us
  Pallas kernels  80.7 us (99%)
    pallas_call x1, Pallas kernels, run_block(): pl.pallas_call(functools.partial(block_kernel, chunks, chunks * LANES), o...  75.3 us
    pallas_call x1, Pallas kernels, finish(): pl.pallas_call(finish_kernel, grid=(steps,), out_shape=(jax.ShapeDtypeStr...  5.33 us

profile of v8, /device:TPU:0, one launch (start us, length us, event | category | flops | bytes accessed | tf_op | source)
XLA Modules:
  0.0 81.3 jit_solution(7340376191630785367)
XLA Ops:
  0.6 75.3 %hyena_block.1 = (s16[2,64,48,128]{3,2,1,0:T(8,128)(2,1)}, s16[4,4,4,9,16,128]{5,4,3,2,1,0:T(8,128)(2,1)}) custom-call(s32[1,128]{1,0:T(1,128)} %tok_mine.1, bf16[512,2048]{1,0:T(8,128)(2,1)} %embedding.1, f32[3,3,4096]{2,1,0:T(4,128)} %conv_taps.1, f32[32,128]{1,0:T(8,128)} %bitcast.12, f32[16,4096]{1,0:T(8,128)} %bitcast.9, f32[16,4096]{1,0:T(8,128)} %bitcast.10, ...), custom_call_target="tpu_custom_call" | custom-call | tf_op jit(solution)/shard_map/hyena_block/pallas_call | solution.py:491
  76.0 5.3 %finish.1 = (f32[512,2048]{1,0:T(8,128)}, f32[4096,128]{1,0:T(8,128)}) custom-call(s16[4,4,4,9,16,128]{5,4,3,2,1,0:T(8,128)(2,1)} %get-tuple-element.6.every.powers, s16[4,4,4,9,16,128]{5,4,3,2,1,0:T(8,128)(2,1)} %get-tuple-element.6.every.powers, s16[128,48,128]{2,1,0:T(8,128)(2,1)} %bitcast.8), custom_call_target="tpu_custom_call" | custom-call | tf_op jit(solution)/shard_map/finish/pallas_call | solution.py:547

commit v9 on v7

--- a/solution.py
+++ b/solution.py
@@ -318,7 +318,7 @@
         hot = jnp.where(low_row == token - bank_of * LANES, 1.0, 0.0).astype(BF16)
         return hot, bank_of
 
-    UNROLL = 16
+    UNROLL = 32
 
     def gather(base, step, carry):
         last_one, last_two = carry
@@ -403,31 +403,35 @@
                 target[pl.ds(base + c, rows, stride=slab), :] = out
             return 0
 
-        lax.fori_loop(0, groups, per_group, 0, unroll=2)
+        lax.fori_loop(0, groups, per_group, 0, unroll=True)
 
     long_conv(mix, long_out, False)
 
-    def emit(place):
-        at = slab_rows(place)
-        q = query[at, :]
-        encode(mixed_out, place, q * long_out[at, :])
-        value_in = real(cot_in[place, :slab, :], cot_in[place, slab:, :])
-        cot[at, :] = value_in
-        mix[at, :] = value_in * q
-
-    def emit_send(place, where):
+    def emit(step, _):
+        for i in range(8):
+            r = step * 8 + i
+            at = slab_rows(r)
+            encode(mixed_out, r, query[at, :] * long_out[at, :])
+        return 0
+
+    def weigh(step, _):
+        for i in range(8):
+            r = step * 8 + i
+            at = slab_rows(r)
+            value_in = real(cot_in[r, :slab, :], cot_in[r, slab:, :])
+            cot[at, :] = value_in
+            mix[at, :] = value_in * query[at, :]
+        return 0
+
+    def send_mixed(place, where):
         send(mixed_out.at[place, sent_rows], mixer.at[me, sent_rows], mixer_sems, where)
 
+    lax.fori_loop(0, rows // 8, emit, 0)
+    each_peer(send_mixed)
+    mixer[me] = mixed_out[me]
     most = pl.ds(0, rows - 1)
     wait_bytes(cot_in.at[most, sent_rows], cot_sems.at[1])
-    def emit_step(step, _):
-        for i in range(8):
-            emit(step * 8 + i)
-        return 0
-
-    lax.fori_loop(0, rows // 8, emit_step, 0)
-    each_peer(emit_send)
-    mixer[me] = mixed_out[me]
+    lax.fori_loop(0, rows // 8, weigh, 0)
 
     grad_mixed = query
     long_conv(mix, grad_mixed, True)
@@ -522,12 +526,15 @@
     )(tok, embedding, conv_taps, gains, residues, decays, seeds, cot)
 
 
-def finish_kernel(every, powers, mixer, grad_out, mixer_out):
-    height = grad_out.shape[0]
+def finish_kernel(every, mixer, grad_out, mixer_out):
+    tiles = every.shape[3] - 1
     for z in range(every.shape[0]):
         for x in range(every.shape[1]):
             n = z * every.shape[1] + x
-            grad_out[:, n * LANES : (n + 1) * LANES] = real(every[z, x, 0].reshape(height, LANES), powers[z, x, 0, 0])
+            for y in range(every.shape[2]):
+                grad_out[y * LANES : (y + 1) * LANES, n * LANES : (n + 1) * LANES] = real(
+                    every[z, x, y, :tiles].reshape(LANES, LANES), every[z, x, y, tiles]
+                )
     slab = mixer.shape[1] - 16
     for n in range(mixer.shape[0]):
         mixer_out[n * slab : (n + 1) * slab, :] = real(mixer[n, :slab, :], mixer[n, slab:, :])
@@ -537,9 +544,8 @@
     a, b, c, tiles, height = every.shape[:5]
     blocks, slab = mixer.shape[0], mixer.shape[1] - 16
     tall = blocks * slab
-    cuts = 1
-    part = (tiles - 1) // cuts
-    steps = c * cuts
+    fold = 2
+    steps = c // fold
     return pl.pallas_call(
         finish_kernel,
         grid=(steps,),
@@ -548,16 +554,15 @@
             jax.ShapeDtypeStruct((tall, LANES), F32),
         ),
         in_specs=[
-            pl.BlockSpec((a, b, 1, part, height, LANES), lambda n: (0, 0, n // cuts, n % cuts, 0, 0)),
-            pl.BlockSpec((a, b, 1, 1, height, LANES), lambda n: (0, 0, n // cuts, tiles - 1, 0, 0)),
+            pl.BlockSpec((a, b, fold, tiles, height, LANES), lambda n: (0, 0, n, 0, 0, 0)),
             pl.BlockSpec((blocks // steps, *mixer.shape[1:]), lambda n: (n, 0, 0)),
         ],
         out_specs=(
-            pl.BlockSpec((LANES // cuts, a * b * LANES), lambda n: (n, 0)),
+            pl.BlockSpec((fold * LANES, a * b * LANES), lambda n: (n, 0)),
             pl.BlockSpec((tall // steps, LANES), lambda n: (n, 0)),
         ),
         name="finish",
-    )(every, every, mixer)
+    )(every, mixer)
 
 
 def body(token_ids, embedding, conv_taps, residues, decays, filter_seed, skip_gain, cotangent):

time: 75.6 us -> 73.5 us (0.972)
  Pallas kernels: 74.7 us -> 72.7 us
    pallas_call x1, Pallas kernels: 69.3 us -> 68.1 us  [run_block(): pl.pallas_call(functools.partial(block_kernel, chunks, chunks * LANES), o...]
    pallas_call x1, Pallas kernels: 5.33 us -> 4.53 us  [finish(): pl.pallas_call(finish_kernel, grid=(steps,), out_shape=(jax.ShapeDtypeStr...]
where the time goes in v9:
time: 73.5 us; the launch traced here: 73.3 us
  Pallas kernels  72.7 us (99%)
    pallas_call x1, Pallas kernels, run_block(): pl.pallas_call(functools.partial(block_kernel, chunks, chunks * LANES), o...  68.1 us
    pallas_call x1, Pallas kernels, finish(): pl.pallas_call(finish_kernel, grid=(steps,), out_shape=(jax.ShapeDtypeStr...  4.53 us

profile of v9, /device:TPU:0, one launch (start us, length us, event | category | flops | bytes accessed | tf_op | source)
XLA Modules:
  0.0 73.3 jit_solution(14748548490554263053)
XLA Ops:
  0.6 68.1 %hyena_block.1 = (s16[128,48,128]{2,1,0:T(8,128)(2,1)}, s16[4,4,4,9,16,128]{5,4,3,2,1,0:T(8,128)(2,1)}) custom-call(s32[1,128]{1,0:T(1,128)} %tok_mine.1, bf16[512,2048]{1,0:T(8,128)(2,1)} %embedding.1, f32[3,3,4096]{2,1,0:T(4,128)} %conv_taps.1, f32[32,128]{1,0:T(8,128)} %bitcast.10, f32[16,4096]{1,0:T(8,128)} %bitcast.7, f32[16,4096]{1,0:T(8,128)} %bitcast.8, ...), custom_call_target="tpu_custom_call" | custom-call | tf_op jit(solution)/shard_map/hyena_block/pallas_call | solution.py:493
  68.8 4.5 %finish.1 = (f32[512,2048]{1,0:T(8,128)}, f32[4096,128]{1,0:T(8,128)}) custom-call(s16[4,4,4,9,16,128]{5,4,3,2,1,0:T(8,128)(2,1)} %get-tuple-element.6.every, s16[128,48,128]{2,1,0:T(8,128)(2,1)} %get-tuple-element.7.mixer), custom_call_target="tpu_custom_call" | custom-call | tf_op jit(solution)/shard_map/finish/pallas_call | solution.py:549

commit v10 on v9

--- a/solution.py
+++ b/solution.py
@@ -408,15 +408,15 @@
     long_conv(mix, long_out, False)
 
     def emit(step, _):
-        for i in range(8):
-            r = step * 8 + i
+        for i in range(32):
+            r = step * 32 + i
             at = slab_rows(r)
             encode(mixed_out, r, query[at, :] * long_out[at, :])
         return 0
 
     def weigh(step, _):
-        for i in range(8):
-            r = step * 8 + i
+        for i in range(16):
+            r = step * 16 + i
             at = slab_rows(r)
             value_in = real(cot_in[r, :slab, :], cot_in[r, slab:, :])
             cot[at, :] = value_in
@@ -426,12 +426,12 @@
     def send_mixed(place, where):
         send(mixed_out.at[place, sent_rows], mixer.at[me, sent_rows], mixer_sems, where)
 
-    lax.fori_loop(0, rows // 8, emit, 0)
+    lax.fori_loop(0, rows // 32, emit, 0)
     each_peer(send_mixed)
     mixer[me] = mixed_out[me]
     most = pl.ds(0, rows - 1)
     wait_bytes(cot_in.at[most, sent_rows], cot_sems.at[1])
-    lax.fori_loop(0, rows // 8, weigh, 0)
+    lax.fori_loop(0, rows // 16, weigh, 0)
 
     grad_mixed = query
     long_conv(mix, grad_mixed, True)

time: 73.5 us -> 73.3 us (level)
  no operation moved by 1% of the time
where the time goes in v10:
time: 73.3 us; the launch traced here: 73.1 us
  Pallas kernels  72.4 us (99%)
    pallas_call x1, Pallas kernels, run_block(): pl.pallas_call(functools.partial(block_kernel, chunks, chunks * LANES), o...  67.9 us
    pallas_call x1, Pallas kernels, finish(): pl.pallas_call(finish_kernel, grid=(steps,), out_shape=(jax.ShapeDtypeStr...  4.53 us

profile of v10, /device:TPU:0, one launch (start us, length us, event | category | flops | bytes accessed | tf_op | source)
XLA Modules:
  0.0 73.1 jit_solution(4652372672740189783)
XLA Ops:
  0.6 67.9 %hyena_block.1 = (s16[128,48,128]{2,1,0:T(8,128)(2,1)}, s16[4,4,4,9,16,128]{5,4,3,2,1,0:T(8,128)(2,1)}) custom-call(s32[1,128]{1,0:T(1,128)} %tok_mine.1, bf16[512,2048]{1,0:T(8,128)(2,1)} %embedding.1, f32[3,3,4096]{2,1,0:T(4,128)} %conv_taps.1, f32[32,128]{1,0:T(8,128)} %bitcast.10, f32[16,4096]{1,0:T(8,128)} %bitcast.7, f32[16,4096]{1,0:T(8,128)} %bitcast.8, ...), custom_call_target="tpu_custom_call" | custom-call | tf_op jit(solution)/shard_map/hyena_block/pallas_call | solution.py:493
  68.5 4.5 %finish.1 = (f32[512,2048]{1,0:T(8,128)}, f32[4096,128]{1,0:T(8,128)}) custom-call(s16[4,4,4,9,16,128]{5,4,3,2,1,0:T(8,128)(2,1)} %get-tuple-element.6.every, s16[128,48,128]{2,1,0:T(8,128)(2,1)} %get-tuple-element.7.mixer), custom_call_target="tpu_custom_call" | custom-call | tf_op jit(solution)/shard_map/finish/pallas_call | solution.py:549

commit v11 on v10

--- a/solution.py
+++ b/solution.py
@@ -177,7 +177,7 @@
                 action(side * chunks + there, (side, there))
             return 0
 
-        lax.fori_loop(1, chunks, step, 0, unroll=7)
+        lax.fori_loop(1, chunks, step, 0, unroll=21)
 
     def send(source, target, sems, where):
         pltpu.make_async_remote_copy(

time: 73.3 us -> 72.6 us (level)
  no operation moved by 1% of the time
where the time goes in v11:
time: 72.6 us; the launch traced here: 72.4 us
  Pallas kernels  71.7 us (99%)
    pallas_call x1, Pallas kernels, run_block(): pl.pallas_call(functools.partial(block_kernel, chunks, chunks * LANES), o...  67.2 us
    pallas_call x1, Pallas kernels, finish(): pl.pallas_call(finish_kernel, grid=(steps,), out_shape=(jax.ShapeDtypeStr...  4.53 us

profile of v11, /device:TPU:0, one launch (start us, length us, event | category | flops | bytes accessed | tf_op | source)
XLA Modules:
  0.0 72.4 jit_solution(9472886783052565029)
XLA Ops:
  0.6 67.2 %hyena_block.1 = (s16[128,48,128]{2,1,0:T(8,128)(2,1)}, s16[4,4,4,9,16,128]{5,4,3,2,1,0:T(8,128)(2,1)}) custom-call(s32[1,128]{1,0:T(1,128)} %tok_mine.1, bf16[512,2048]{1,0:T(8,128)(2,1)} %embedding.1, f32[3,3,4096]{2,1,0:T(4,128)} %conv_taps.1, f32[32,128]{1,0:T(8,128)} %bitcast.10, f32[16,4096]{1,0:T(8,128)} %bitcast.7, f32[16,4096]{1,0:T(8,128)} %bitcast.8, ...), custom_call_target="tpu_custom_call" | custom-call | tf_op jit(solution)/shard_map/hyena_block/pallas_call | solution.py:493
  67.8 4.5 %finish.1 = (f32[512,2048]{1,0:T(8,128)}, f32[4096,128]{1,0:T(8,128)}) custom-call(s16[4,4,4,9,16,128]{5,4,3,2,1,0:T(8,128)(2,1)} %get-tuple-element.6.every, s16[128,48,128]{2,1,0:T(8,128)(2,1)} %get-tuple-element.7.mixer), custom_call_target="tpu_custom_call" | custom-call | tf_op jit(solution)/shard_map/finish/pallas_call | solution.py:549
